TPU v7x, 256 devices: a whole 4x4x8 slice. The times are simulated.
256 devices in a mesh: leaf: 32 (over y, x, core), front: 8 (over z).
Axes of the slice: x: 4, y: 4, z: 8, core: 2. Of those that a mesh axis runs over, the one named last changes fastest.
Arguments:
- leaf_contrib: float32 [32768, 1024], P(('leaf', 'front')), may hold values from -1 to 7, as said below
- entries_lower: float32 [32768, 1024], P(('leaf', 'front')), may hold values from -1 to 4, as said below
- entries_middle: float32 [16384, 1024], P(('leaf', 'front')), may hold values from -1 to 4, as said below
- entries_upper: float32 [8192, 1024], P(('leaf', 'front')), may hold values from -1 to 4, as said below
- assembly_lower: int32 [16, 2, 8], replicated, may hold values from 0 to 15, as said below
- assembly_middle: int32 [8, 2, 8], replicated, may hold values from 0 to 15, as said below
- assembly_upper: int32 [4, 2, 8], replicated, may hold values from 0 to 15, as said below
Outputs:
- factor_lower: float32 [32768, 1024], P(('leaf', 'front'))
- factor_middle: float32 [16384, 1024], P(('leaf', 'front'))
- factor_upper: float32 [8192, 1024], P(('leaf', 'front'))
- top_update: float32 [4096, 1024], P(('leaf', 'front'))
Inputs may be any that keep to these rules, and one draw needn't show every extreme that they name: `leaf_contrib`: in natural row order each leaf's block is symmetric positive definite. `entries_lower`: in natural row order the first 1024 rows of each front's entries form a symmetric positive definite block. `entries_middle`: in natural row order the first 1024 rows of each front's entries form a symmetric positive definite block. `entries_upper`: in natural row order the first 1024 rows of each front's entries form a symmetric positive definite block. `assembly_lower`: each child's block j goes to parent block j or j + 8, and at least one of the two children sends its block j to j + 8. `assembly_middle`: each child's block j goes to parent block j or j + 8, and at least one of the two children sends its block j to j + 8. `assembly_upper`: each child's block j goes to parent block j or j + 8, and at least one of the two children sends its block j to j + 8.
All inputs are finite; a program needn't handle non-finite values.
Results may differ from a plain program's by a relative error of at most 0.0003.
Values sent between devices are 32-bit elements; how exact they have to be, the bound alone decides.
A program may use at most 128 MiB of HBM per device.

v0:
```python
import jax
import jax.numpy as jnp
from jax import lax
from jax.sharding import PartitionSpec as P

BLK = 128
PIVOT_BLOCKS = 8


def partner_2(value, axis, stride):
    mask = 2**stride
    pairs = [(source, source ^ mask) for source in range(lax.axis_size(axis))]
    return lax.ppermute(value, axis, pairs)


def product(left, right):
    return jnp.dot(left, right, precision=lax.Precision.HIGHEST, preferred_element_type=jnp.float32)


def factor_inverse(matrix):
    order_size = matrix.shape[0]
    if order_size <= 128 or order_size % 2 != 0:
        lower_factor = jnp.linalg.cholesky(matrix)
        identity = jnp.eye(order_size, dtype=jnp.float32)
        inverse = jax.scipy.linalg.solve_triangular(lower_factor, identity, lower=True)
        return (lower_factor, inverse)
    half = order_size // 2
    first_factor, first_inverse = factor_inverse(matrix[:half, :half])
    coupling = product(matrix[half:, :half], first_inverse.T)
    second_factor, second_inverse = factor_inverse(
        matrix[half:, half:] - product(coupling, coupling.T)
    )
    corner = -product(second_inverse, product(coupling, first_inverse))
    zeros_block = jnp.zeros((half, half), jnp.float32)
    lower_factor = jnp.concatenate(
        [
            jnp.concatenate([first_factor, zeros_block], 1),
            jnp.concatenate([coupling, second_factor], 1),
        ],
        0,
    )
    inverse = jnp.concatenate(
        [
            jnp.concatenate([first_inverse, zeros_block], 1),
            jnp.concatenate([corner, second_inverse], 1),
        ],
        0,
    )
    return (lower_factor, inverse)


def reversed_bits(number, bit_count):
    result = jnp.zeros((), jnp.int32)
    for bit_index in range(bit_count):
        result = result + (number >> bit_index & 1) * (1 << bit_count - 1 - bit_index)
    return result


def join_pieces(mine, theirs, bit_index, axis_index):
    upper_bit = lax.axis_index("leaf") >> bit_index & 1
    return jnp.where(
        upper_bit == 0,
        jnp.concatenate([mine, theirs], axis_index),
        jnp.concatenate([theirs, mine], axis_index),
    )


def group_gather(pieces, height):
    gathered = lax.all_gather(pieces[:, None], "front", axis=1, tiled=True)
    for bit_index in reversed(range(height)):
        partner = partner_2(gathered, "leaf", bit_index)
        gathered = join_pieces(gathered, partner, bit_index, 2)
    return gathered


def spread_columns(rows_in, upper_mask):
    blocks = rows_in.reshape(rows_in.shape[0], rows_in.shape[1], upper_mask.shape[0], -1)
    to_pivot = blocks * (1.0 - upper_mask)[None, None, :, None]
    to_update = blocks * upper_mask[None, None, :, None]
    return jnp.concatenate([to_pivot, to_update], axis=2).reshape(
        rows_in.shape[0], rows_in.shape[1], -1
    )


def own_rows(whole, front_index, piece_index, piece_rows):
    chosen = lax.dynamic_index_in_dim(whole, front_index, 1, keepdims=False)
    return lax.dynamic_slice_in_dim(chosen, piece_index * piece_rows, piece_rows, 1)


def local(
    leaf_contrib,
    entries_lower,
    entries_middle,
    entries_upper,
    assembly_lower,
    assembly_middle,
    assembly_upper,
):
    front_count = lax.axis_size("front")
    local_count = PIVOT_BLOCKS // front_count
    leaf_index = lax.axis_index("leaf")
    front_index = lax.axis_index("front")
    pivot_size = leaf_contrib.shape[1]
    update = leaf_contrib.reshape(local_count, BLK, pivot_size)
    my_blocks = front_index + front_count * jnp.arange(local_count, dtype=jnp.int32)
    selector = (jnp.arange(PIVOT_BLOCKS, dtype=jnp.int32)[None, :] == my_blocks[:, None]).astype(
        jnp.float32
    )
    results = []
    for height, entries, routes in (
        (1, entries_lower, assembly_lower),
        (2, entries_middle, assembly_middle),
        (3, entries_upper, assembly_upper),
    ):
        piece_rows = BLK // 2**height
        child_bit = leaf_index >> height - 1 & 1
        low_rows = update[:, :piece_rows]
        high_rows = update[:, piece_rows:]
        kept = jnp.where(child_bit == 0, low_rows, high_rows)
        outgoing = jnp.where(child_bit == 0, high_rows, low_rows)
        received = partner_2(outgoing, "leaf", height - 1)
        route_pair = lax.dynamic_index_in_dim(routes, leaf_index >> height, 0, keepdims=False)
        upper_masks = (route_pair >= PIVOT_BLOCKS).astype(jnp.float32)
        own_mask = jnp.where(child_bit == 0, upper_masks[0], upper_masks[1])
        other_mask = jnp.where(child_bit == 0, upper_masks[1], upper_masks[0])
        slab_rows = local_count * piece_rows
        pivot_slab = entries[:slab_rows].reshape(local_count, piece_rows, pivot_size)
        update_slab = jnp.zeros((local_count, piece_rows, 2 * pivot_size), jnp.float32)
        update_slab = update_slab.at[:, :, :pivot_size].set(
            entries[slab_rows:].reshape(local_count, piece_rows, pivot_size)
        )
        for contribution, column_mask in ((kept, own_mask), (received, other_mask)):
            spread = spread_columns(contribution, column_mask)
            row_upper = jnp.sum(selector * column_mask[None, :], axis=1)
            pivot_slab = pivot_slab + (1.0 - row_upper)[:, None, None] * spread[:, :, :pivot_size]
            update_slab = update_slab + row_upper[:, None, None] * spread
        piece_index = reversed_bits(leaf_index & 2**height - 1, height)
        update_pivot = update_slab[:, :, :pivot_size]
        whole_pivot = group_gather(pivot_slab, height).reshape(pivot_size, pivot_size)
        lower_factor, factor_inv = factor_inverse(whole_pivot)
        own_panel = product(update_pivot.reshape(-1, pivot_size), factor_inv.T)
        all_panel = group_gather(
            own_panel.reshape(local_count, piece_rows, pivot_size), height
        ).reshape(pivot_size, pivot_size)
        own_factor = own_rows(
            lower_factor.reshape(local_count, front_count, BLK, pivot_size),
            front_index,
            piece_index,
            piece_rows,
        ).reshape(-1, pivot_size)
        results.append(jnp.concatenate([own_factor, own_panel], axis=0))
        schur_rows = update_slab[:, :, pivot_size:].reshape(-1, pivot_size) - product(
            own_panel, all_panel.T
        )
        update = schur_rows.reshape(local_count, piece_rows, pivot_size)
    return (results[0], results[1], results[2], update.reshape(-1, pivot_size))


def solution(mesh):
    in_specs = (
        P(("leaf", "front"), None),
        P(("leaf", "front"), None),
        P(("leaf", "front"), None),
        P(("leaf", "front"), None),
        P(),
        P(),
        P(),
    )
    out_specs = (
        P(("leaf", "front"), None),
        P(("leaf", "front"), None),
        P(("leaf", "front"), None),
        P(("leaf", "front"), None),
    )
    return jax.shard_map(local, mesh=mesh, in_specs=in_specs, out_specs=out_specs, check_vma=False)
```

profile of v0, /device:TPU:1, one launch (start us, length us, event | category | flops | bytes accessed | tf_op | source)
XLA Modules:
  0.0 1222.6 jit_solution(8824010916489031496)
XLA Ops:
  16.0 38.2 %all-gather.11.cloned.1.call-done = f32[8,64,1024]{2,1,0:T(8,128)} async-done(((f32[1,64,1024]{2,1,0:T(8,128)}), f32[8,64,1024]{2,1,0:T(8,128)}) %all-gather.11.cloned.1.call-update) | async-done | bytes 2097168 | tf_op jit(solution)/shard_map/all_gather | solution.py:69
  68.6 11.7 cholesky.374
  82.2 9.8 custom-call.28
  95.2 11.7 cholesky.385
  108.9 10.0 custom-call.29
  122.0 11.7 cholesky.396
  135.6 9.8 custom-call.30
  148.6 11.9 cholesky.407
  162.4 9.8 custom-call.31
  180.1 12.1 cholesky.418
  194.2 9.8 custom-call.32
  205.2 11.7 cholesky.429
  218.9 9.8 custom-call.33
  230.5 11.9 cholesky.440
  244.3 9.8 custom-call.34
  265.1 12.1 cholesky.451
  279.1 10.4 custom-call.35
  298.3 8.6 fusion.12
  307.0 35.7 %all-gather.13.cloned.1.call-done = f32[512,1024]{1,0:T(8,128)} async-done(((f32[64,1024]{1,0:T(8,128)}), f32[512,1024]{1,0:T(8,128)}) %all-gather.13.cloned.1.call-update) | async-done | bytes 2097168 | tf_op jit(solution)/shard_map/all_gather | solution.py:69
  364.3 32.8 %all-gather.15.cloned.1.call-done = f32[8,32,1024]{2,1,0:T(8,128)} async-done(((f32[1,32,1024]{2,1,0:T(8,128)}), f32[8,32,1024]{2,1,0:T(8,128)}) %all-gather.15.cloned.1.call-update) | async-done | bytes 1048592 | tf_op jit(solution)/shard_map/all_gather | solution.py:69
  398.3 17.9 %collective-permute-done.4 = f32[1,8,32,1024]{3,2,1,0:T(8,128)S(1)} collective-permute-done((f32[1,8,32,1024]{3,2,1,0:T(8,128)}, f32[1,8,32,1024]{3,2,1,0:T(8,128)S(1)}, u32[]{:S(2)}, u32[]{:S(2)}) %collective-permute-start.4) | collective-permute-done | bytes 1048608 | tf_op jit(solution)/shard_map/ppermute | solution.py:13
  418.0 7.0 collective-permute-start.5
  432.5 11.7 cholesky.462
  446.2 9.8 custom-call.36
  459.2 11.7 cholesky.473
  472.9 10.0 custom-call.37
  486.0 11.7 cholesky.484
  499.6 9.8 custom-call.38
  513.6 12.1 cholesky.495
  527.7 9.8 custom-call.39
  548.5 11.9 cholesky.506
  562.3 9.8 custom-call.40
  575.0 11.7 cholesky.517
  588.7 9.8 custom-call.41
  606.6 13.6 %cholesky.528 = f32[128,128]{1,0:T(8,128)} custom-call(f32[128,128]{1,0:T(8,128)} %fusion.248), custom_call_target="Cholesky" | custom-call | tf_op jit(solution)/shard_map/jit(cholesky)/cholesky | solution.py:23
  623.9 11.3 custom-call.42
  648.3 11.9 cholesky.539
  662.1 9.8 custom-call.43
  679.2 8.4 fusion.6
  687.6 32.6 %all-gather.17.cloned.1.call-done = f32[256,1024]{1,0:T(8,128)} async-done(((f32[32,1024]{1,0:T(8,128)}), f32[256,1024]{1,0:T(8,128)}) %all-gather.17.cloned.1.call-update) | async-done | bytes 1048592 | tf_op jit(solution)/shard_map/all_gather | solution.py:69
  721.4 17.9 %collective-permute-done.6 = f32[1,8,32,1024]{3,2,1,0:T(8,128)S(1)} collective-permute-done((f32[1,8,32,1024]{3,2,1,0:T(8,128)}, f32[1,8,32,1024]{3,2,1,0:T(8,128)S(1)}, u32[]{:S(2)}, u32[]{:S(2)}) %collective-permute-start.6) | collective-permute-done | bytes 1048608 | tf_op jit(solution)/shard_map/ppermute | solution.py:13
  766.9 19.8 %all-gather.4 = f32[8,16,1024]{2,1,0:T(8,128)S(1)} all-gather(f32[1,16,1024]{2,1,0:T(8,128)S(1)} %get-tuple-element.121), channel_id=6, replica_groups=mesh['leaf'=32,'front'=8] {'front'}, dimensions={0}, use_global_device_ids=true | all-gather | bytes 589824 | tf_op jit(solution)/shard_map/all_gather | solution.py:69
  789.4 6.8 collective-permute-done.9
  797.8 21.0 %collective-permute-done.10 = f32[1,8,32,1024]{3,2,1,0:T(8,128)S(1)} collective-permute-done((f32[1,8,32,1024]{3,2,1,0:T(8,128)S(1)}, f32[1,8,32,1024]{3,2,1,0:T(8,128)S(1)}, u32[]{:S(2)}, u32[]{:S(2)}) %collective-permute-start.10) | collective-permute-done | bytes 1048608 | tf_op jit(solution)/shard_map/ppermute | solution.py:13
  819.0 8.6 collective-permute-start.11
  835.3 11.7 cholesky.550
  848.9 9.8 custom-call.44
  862.0 11.7 cholesky.561
  875.6 10.0 custom-call.45
  890.4 11.7 cholesky.572
  904.0 9.8 custom-call.46
  921.8 11.9 cholesky.583
  935.7 9.8 custom-call.47
  961.6 12.9 %cholesky.594 = f32[128,128]{1,0:T(8,128)S(1)} custom-call(f32[128,128]{1,0:T(8,128)} %fusion.236), custom_call_target="Cholesky" | custom-call | tf_op jit(solution)/shard_map/jit(cholesky)/cholesky | solution.py:23
  976.4 11.3 custom-call.48
  995.6 13.2 %cholesky.605 = f32[128,128]{1,0:T(8,128)} custom-call(f32[128,128]{1,0:T(8,128)} %fusion.234), custom_call_target="Cholesky" | custom-call | tf_op jit(solution)/shard_map/jit(cholesky)/cholesky | solution.py:23
  1012.5 11.3 custom-call.49
  1036.8 13.3 %cholesky.616 = f32[128,128]{1,0:T(8,128)} custom-call(f32[128,128]{1,0:T(8,128)} %fusion.232), custom_call_target="Cholesky" | custom-call | tf_op jit(solution)/shard_map/jit(cholesky)/cholesky | solution.py:23
  1053.8 11.3 custom-call.50
  1080.8 12.7 %cholesky.627 = f32[128,128]{1,0:T(8,128)S(1)} custom-call(f32[128,128]{1,0:T(8,128)} %fusion.230), custom_call_target="Cholesky" | custom-call | tf_op jit(solution)/shard_map/jit(cholesky)/cholesky | solution.py:23
  1095.5 11.3 custom-call.51
  1115.5 7.4 fusion
  1123.5 21.8 %all-gather.5 = f32[128,1024]{1,0:T(8,128)} all-gather(f32[16,1024]{1,0:T(8,128)S(1)} %fusion), channel_id=7, replica_groups=mesh['leaf'=32,'front'=8] {'front'}, dimensions={0}, use_global_device_ids=true | all-gather | bytes 589824 | tf_op jit(solution)/shard_map/all_gather | solution.py:69
  1183.8 7.2 collective-permute-start.14
  (643 shorter events, 375.6 us)
Async XLA Ops:
  7.2 47.1 %all-gather.11.cloned.1.call-start = ((), (), s32[]{:S(2)}) async-start(), calls=%async_computation | async-start | bytes 2359296 | tf_op jit(solution)/shard_map/all_gather | solution.py:69
  8.3 6.4 collective-permute-start
  16.0 326.7 %all-gather.13.cloned.1.call-start = ((), (), s32[]{:S(2)}) async-start(), calls=%async_computation.1 | async-start | bytes 2359296 | tf_op jit(solution)/shard_map/all_gather | solution.py:69
  54.2 8.4 collective-permute-start.1
  119.6 54.9 %copy-start.53 = (f32[256,256]{1,0:T(8,128)}, f32[256,256]{1,0:T(8,128)S(1)}, u32[]{:S(2)}) copy-start(f32[256,256]{1,0:T(8,128)S(1)} %select_maximum_fusion.25) | copy-start | bytes 786436
  146.0 27.4 %copy-start.20 = (f32[128,128]{0,1:T(8,128)}, f32[128,128]{0,1:T(8,128)S(1)}, u32[]{:S(2)}) copy-start(f32[128,128]{0,1:T(8,128)S(1)} %fusion.225) | copy-start | bytes 196612
  180.0 79.2 %copy-start.44 = (f32[128,256]{1,0:T(8,128)S(1)}, f32[128,256]{1,0:T(8,128)}, u32[]{:S(2)}) copy-start(f32[128,256]{1,0:T(8,128)} %copy-done.43) | copy-start | bytes 393220
  204.5 58.7 %copy-start.22 = (f32[128,128]{0,1:T(8,128)}, f32[128,128]{0,1:T(8,128)S(1)}, u32[]{:S(2)}) copy-start(f32[128,128]{0,1:T(8,128)S(1)} %fusion.223) | copy-start | bytes 196612
  229.8 60.9 %copy-start.5 = (f32[256,256]{0,1:T(8,128)}, f32[256,256]{0,1:T(8,128)S(1)}, u32[]{:S(2)}) copy-start(f32[256,256]{0,1:T(8,128)S(1)} %fusion.163) | copy-start | bytes 786436
  254.6 43.6 %copy-start.23 = (f32[128,128]{0,1:T(8,128)}, f32[128,128]{0,1:T(8,128)S(1)}, u32[]{:S(2)}) copy-start(f32[128,128]{0,1:T(8,128)S(1)} %fusion.221) | copy-start | bytes 196612
  259.2 39.1 %copy-start.45 = (f32[1,64,2048]{2,1,0:T(8,128)S(1)}, f32[1,64,2048]{2,1,0:T(8,128)}, u32[]{:S(2)}) copy-start(f32[1,64,2048]{2,1,0:T(8,128)} %multiply_add_fusion) | copy-start | bytes 1572868
  259.2 39.1 %copy-start.58 = (f32[512,512]{1,0:T(8,128)S(1)}, f32[512,512]{1,0:T(8,128)}, u32[]{:S(2)}) copy-start(f32[512,512]{1,0:T(8,128)} %select_maximum_fusion.13) | copy-start | bytes 3145732
  263.2 35.0 %copy-start.86 = (f32[128,256]{1,0:T(8,128)S(1)}, f32[128,256]{1,0:T(8,128)}, u32[]{:S(2)}) copy-start(f32[128,256]{1,0:T(8,128)} %concatenate.730) | copy-start | bytes 393220
  306.9 90.2 %all-gather.15.cloned.1.call-start = ((), (), s32[]{:S(2)}) async-start(), calls=%async_computation.2 | async-start | bytes 1179648 | tf_op jit(solution)/shard_map/all_gather | solution.py:69
  342.7 8.4 collective-permute-start.2
  358.4 4.8 collective-permute-start.3
  364.2 356.0 %all-gather.17.cloned.1.call-start = ((), (), s32[]{:S(2)}) async-start(), calls=%async_computation.3 | async-start | bytes 1179648 | tf_op jit(solution)/shard_map/all_gather | solution.py:69
  397.1 19.1 %collective-permute-start.4 = (f32[1,8,32,1024]{3,2,1,0:T(8,128)}, f32[1,8,32,1024]{3,2,1,0:T(8,128)S(1)}, u32[]{:S(2)}, u32[]{:S(2)}) collective-permute-start(f32[1,8,32,1024]{3,2,1,0:T(8,128)} %bitcast.535), channel_id=1, source_target_pairs={{0,16},{8,24},{16,0},{24,8},{32,48},{40,56},{48,32},{56,40},{64,80... | collective-permute-start | bytes 3145736 | tf_op jit(solution)/shard_map/ppermute | solution.py:13
  418.0 10.7 collective-permute-start.5
  457.4 56.1 %copy-start.24 = (f32[128,128]{0,1:T(8,128)}, f32[128,128]{0,1:T(8,128)S(1)}, u32[]{:S(2)}) copy-start(f32[128,128]{0,1:T(8,128)S(1)} %fusion.219) | copy-start | bytes 196612
  483.6 56.1 %copy-start.54 = (f32[256,256]{1,0:T(8,128)}, f32[256,256]{1,0:T(8,128)S(1)}, u32[]{:S(2)}) copy-start(f32[256,256]{1,0:T(8,128)S(1)} %select_maximum_fusion.21) | copy-start | bytes 786436
  485.0 53.5 %copy-start.6 = (f32[256,256]{0,1:T(8,128)}, f32[256,256]{0,1:T(8,128)S(1)}, u32[]{:S(2)}) copy-start(f32[256,256]{0,1:T(8,128)S(1)} %fusion.160) | copy-start | bytes 786436
  510.0 28.6 %copy-start.26 = (f32[128,128]{0,1:T(8,128)}, f32[128,128]{0,1:T(8,128)S(1)}, u32[]{:S(2)}) copy-start(f32[128,128]{0,1:T(8,128)S(1)} %fusion.217) | copy-start | bytes 196612
  510.6 29.1 %copy-start.40 = (f32[128,256]{1,0:T(8,128)}, f32[128,256]{1,0:T(8,128)S(1)}, u32[]{:S(2)}) copy-start(f32[128,256]{1,0:T(8,128)S(1)} %concatenate.760) | copy-start | bytes 393220
  547.4 97.1 %copy-start.41 = (f32[128,256]{1,0:T(8,128)S(1)}, f32[128,256]{1,0:T(8,128)}, u32[]{:S(2)}) copy-start(f32[128,256]{1,0:T(8,128)} %copy-done.40) | copy-start | bytes 393220
  547.4 97.1 %copy-start.51 = (f32[256,256]{1,0:T(8,128)S(1)}, f32[256,256]{1,0:T(8,128)}, u32[]{:S(2)}) copy-start(f32[256,256]{1,0:T(8,128)} %copy-done.50) | copy-start | bytes 786436
  547.4 97.1 %copy-start.55 = (f32[256,256]{1,0:T(8,128)S(1)}, f32[256,256]{1,0:T(8,128)}, u32[]{:S(2)}) copy-start(f32[256,256]{1,0:T(8,128)} %copy-done.54) | copy-start | bytes 786436
  573.4 25.4 %copy-start.28 = (f32[128,128]{0,1:T(8,128)}, f32[128,128]{0,1:T(8,128)S(1)}, u32[]{:S(2)}) copy-start(f32[128,128]{0,1:T(8,128)S(1)} %fusion.215) | copy-start | bytes 196612
  598.9 25.0 %copy-start.66 = (f32[128,128]{1,0:T(8,128)}, f32[128,128]{1,0:T(8,128)S(1)}, u32[]{:S(2)}) copy-start(f32[128,128]{1,0:T(8,128)S(1)} %copy.167) | copy-start | bytes 196612
  599.2 36.0 %copy-start.63 = (f32[128,128]{1,0:T(8,128)}, f32[128,128]{1,0:T(8,128)S(1)}, u32[]{:S(2)}) copy-start(f32[128,128]{1,0:T(8,128)S(1)} %convolution_negate_fusion.14) | copy-start | bytes 196612
  600.5 71.7 %copy-start.8 = (f32[256,256]{0,1:T(8,128)}, f32[256,256]{0,1:T(8,128)S(1)}, u32[]{:S(2)}) copy-start(f32[256,256]{0,1:T(8,128)S(1)} %fusion.158) | copy-start | bytes 786436
  637.3 41.8 %copy-start.30 = (f32[128,128]{0,1:T(8,128)}, f32[128,128]{0,1:T(8,128)S(1)}, u32[]{:S(2)}) copy-start(f32[128,128]{0,1:T(8,128)S(1)} %fusion.213) | copy-start | bytes 196612
  648.2 30.9 %copy-start.82 = (f32[1,32,2048]{2,1,0:T(8,128)S(1)}, f32[1,32,2048]{2,1,0:T(8,128)}, u32[]{:S(2)}) copy-start(f32[1,32,2048]{2,1,0:T(8,128)} %multiply_add_fusion.1) | copy-start | bytes 786436
  648.2 30.9 %copy-start.87 = (f32[128,256]{1,0:T(8,128)S(1)}, f32[128,256]{1,0:T(8,128)}, u32[]{:S(2)}) copy-start(f32[128,256]{1,0:T(8,128)} %concatenate.781) | copy-start | bytes 393220
  720.2 19.1 %collective-permute-start.6 = (f32[1,8,32,1024]{3,2,1,0:T(8,128)}, f32[1,8,32,1024]{3,2,1,0:T(8,128)S(1)}, u32[]{:S(2)}, u32[]{:S(2)}) collective-permute-start(f32[1,8,32,1024]{3,2,1,0:T(8,128)} %bitcast.537), channel_id=1, source_target_pairs={{0,16},{8,24},{16,0},{24,8},{32,48},{40,56},{48,32},{56,40},{64,80... | collective-permute-start | bytes 3145736 | tf_op jit(solution)/shard_map/ppermute | solution.py:13
  742.6 10.8 collective-permute-start.7
  761.9 4.7 collective-permute-start.8
  766.8 29.4 %copy-start.69 = (f32[1,16,2048]{2,1,0:T(8,128)}, f32[1,16,2048]{2,1,0:T(8,128)S(1)}, u32[]{:S(2)}) copy-start(f32[1,16,2048]{2,1,0:T(8,128)S(1)} %reshape.1335) | copy-start | bytes 393220
  766.8 29.4 %copy-start.71 = (f32[1,16,2048]{2,1,0:T(8,128)}, f32[1,16,2048]{2,1,0:T(8,128)S(1)}, u32[]{:S(2)}) copy-start(f32[1,16,2048]{2,1,0:T(8,128)S(1)} %get-tuple-element.120) | copy-start | bytes 393220
  786.7 9.5 collective-permute-start.9
  796.4 31.3 %copy-start.70 = (f32[1,16,2048]{2,1,0:T(8,128)S(1)}, f32[1,16,2048]{2,1,0:T(8,128)}, u32[]{:S(2)}) copy-start(f32[1,16,2048]{2,1,0:T(8,128)} %copy-done.69) | copy-start | bytes 393220
  796.4 31.3 %copy-start.72 = (f32[1,16,2048]{2,1,0:T(8,128)S(1)}, f32[1,16,2048]{2,1,0:T(8,128)}, u32[]{:S(2)}) copy-start(f32[1,16,2048]{2,1,0:T(8,128)} %copy-done.71) | copy-start | bytes 393220
  796.4 22.4 %collective-permute-start.10 = (f32[1,8,32,1024]{3,2,1,0:T(8,128)S(1)}, f32[1,8,32,1024]{3,2,1,0:T(8,128)S(1)}, u32[]{:S(2)}, u32[]{:S(2)}) collective-permute-start(f32[1,8,32,1024]{3,2,1,0:T(8,128)S(1)} %maximum_select_fusion.11), channel_id=1, source_target_pairs={{0,16},{8,24},{16,0},{24,8},{32,48},{40,56},{48,32},{56,40},{64,80... | collective-permute-start | bytes 3145736 | tf_op jit(solution)/shard_map/ppermute | solution.py:13
  819.0 12.4 %collective-permute-start.11 = (f32[1,8,64,1024]{3,2,1,0:T(8,128)S(1)}, f32[1,8,64,1024]{3,2,1,0:T(8,128)S(1)}, u32[]{:S(2)}, u32[]{:S(2)}) collective-permute-start(f32[1,8,64,1024]{3,2,1,0:T(8,128)S(1)} %maximum_select_fusion.8), channel_id=1, source_target_pairs={{0,8},{8,0},{16,24},{24,16},{32,40},{40,32},{48,56},{56,48},{64,72... | collective-permute-start | bytes 6291464 | tf_op jit(solution)/shard_map/ppermute | solution.py:13
  860.2 26.1 %copy-start.32 = (f32[128,128]{0,1:T(8,128)}, f32[128,128]{0,1:T(8,128)S(1)}, u32[]{:S(2)}) copy-start(f32[128,128]{0,1:T(8,128)S(1)} %fusion.209) | copy-start | bytes 196612
  886.3 61.1 %copy-start.56 = (f32[256,256]{1,0:T(8,128)}, f32[256,256]{1,0:T(8,128)S(1)}, u32[]{:S(2)}) copy-start(f32[256,256]{1,0:T(8,128)S(1)} %select_maximum_fusion.17) | copy-start | bytes 786436
  887.8 59.7 %copy-start.10 = (f32[256,256]{0,1:T(8,128)}, f32[256,256]{0,1:T(8,128)S(1)}, u32[]{:S(2)}) copy-start(f32[256,256]{0,1:T(8,128)S(1)} %fusion.156) | copy-start | bytes 786436
  914.3 33.1 %copy-start.34 = (f32[128,128]{0,1:T(8,128)}, f32[128,128]{0,1:T(8,128)S(1)}, u32[]{:S(2)}) copy-start(f32[128,128]{0,1:T(8,128)S(1)} %fusion.207) | copy-start | bytes 196612
  916.2 31.3 %copy-start.42 = (f32[128,256]{1,0:T(8,128)}, f32[128,256]{1,0:T(8,128)S(1)}, u32[]{:S(2)}) copy-start(f32[128,256]{1,0:T(8,128)S(1)} %concatenate.820) | copy-start | bytes 393220
  1115.5 33.9 %copy-start.21 = (f32[128,128]{0,1:T(8,128)S(1)}, f32[128,128]{0,1:T(8,128)}, u32[]{:S(2)}) copy-start(f32[128,128]{0,1:T(8,128)} %copy-done.20) | copy-start | bytes 196612
  1145.3 13.5 %collective-permute-start.12 = (f32[1,8,16,1024]{3,2,1,0:T(8,128)}, f32[1,8,16,1024]{3,2,1,0:T(8,128)}, u32[]{:S(2)}, u32[]{:S(2)}) collective-permute-start(f32[1,8,16,1024]{3,2,1,0:T(8,128)} %bitcast.118), channel_id=1, source_target_pairs={{0,32},{8,40},{16,48},{24,56},{32,0},{40,8},{48,16},{56,24},{64,96... | collective-permute-start | bytes 1572872 | tf_op jit(solution)/shard_map/ppermute | solution.py:13
  1149.4 12.3 %copy-start.90 = (f32[128,128]{1,0:T(8,128)S(1)}, f32[128,128]{1,0:T(8,128)}, u32[]{:S(2)}) copy-start(f32[128,128]{1,0:T(8,128)} %get-tuple-element.85) | copy-start | bytes 196612
  1150.1 11.6 copy-start.91
  1161.5 19.0 %collective-permute-start.13 = (f32[1,8,32,1024]{3,2,1,0:T(8,128)}, f32[1,8,32,1024]{3,2,1,0:T(8,128)}, u32[]{:S(2)}, u32[]{:S(2)}) collective-permute-start(f32[1,8,32,1024]{3,2,1,0:T(8,128)} %maximum_select_fusion.13), channel_id=1, source_target_pairs={{0,16},{8,24},{16,0},{24,8},{32,48},{40,56},{48,32},{56,40},{64,80... | collective-permute-start | bytes 3145736 | tf_op jit(solution)/shard_map/ppermute | solution.py:13
  1171.0 20.0 %copy-start.14 = (f32[512,512]{1,0:T(8,128)S(1)}, f32[512,512]{1,0:T(8,128)}, u32[]{:S(2)}) copy-start(f32[512,512]{1,0:T(8,128)} %copy.174) | copy-start | bytes 3145732
  1171.0 20.0 %copy-start.67 = (f32[256,256]{1,0:T(8,128)S(1)}, f32[256,256]{1,0:T(8,128)}, u32[]{:S(2)}) copy-start(f32[256,256]{1,0:T(8,128)} %copy.173) | copy-start | bytes 786436
  1171.0 20.0 %copy-start.92 = (f32[128,128]{1,0:T(8,128)S(1)}, f32[128,128]{1,0:T(8,128)}, u32[]{:S(2)}) copy-start(f32[128,128]{1,0:T(8,128)} %get-tuple-element.65) | copy-start | bytes 196612
  1171.0 20.0 %copy-start.93 = (f32[128,128]{1,0:T(8,128)S(1)}, f32[128,128]{1,0:T(8,128)}, u32[]{:S(2)}) copy-start(f32[128,128]{1,0:T(8,128)} %get-tuple-element.63) | copy-start | bytes 196612
  1183.8 12.0 copy-start.48
  1183.8 12.8 %copy-start.37 = (f32[128,128]{0,1:T(8,128)S(1)}, f32[128,128]{0,1:T(8,128)}, u32[]{:S(2)}) copy-start(f32[128,128]{0,1:T(8,128)} %copy-done.36) | copy-start | bytes 196612
  1183.8 12.9 %copy-start.33 = (f32[128,128]{0,1:T(8,128)S(1)}, f32[128,128]{0,1:T(8,128)}, u32[]{:S(2)}) copy-start(f32[128,128]{0,1:T(8,128)} %copy-done.32) | copy-start | bytes 196612
  1183.8 13.0 %copy-start.35 = (f32[128,128]{0,1:T(8,128)S(1)}, f32[128,128]{0,1:T(8,128)}, u32[]{:S(2)}) copy-start(f32[128,128]{0,1:T(8,128)} %copy-done.34) | copy-start | bytes 196612
  1183.8 13.7 %copy-start.11 = (f32[256,256]{0,1:T(8,128)S(1)}, f32[256,256]{0,1:T(8,128)}, u32[]{:S(2)}) copy-start(f32[256,256]{0,1:T(8,128)} %copy-done.10) | copy-start | bytes 786436
  1183.8 23.1 %collective-permute-start.14 = (f32[1,8,64,1024]{3,2,1,0:T(8,128)}, f32[1,8,64,1024]{3,2,1,0:T(8,128)}, u32[]{:S(2)}, u32[]{:S(2)}) collective-permute-start(f32[1,8,64,1024]{3,2,1,0:T(8,128)} %maximum_select_fusion.9), channel_id=1, source_target_pairs={{0,8},{8,0},{16,24},{24,16},{32,40},{40,32},{48,56},{56,48},{64,72... | collective-permute-start | bytes 6291464 | tf_op jit(solution)/shard_map/ppermute | solution.py:13
  (61 other events, 271.1 us)
Sparse Core Ops, SparseCore 0:
  16.1 38.1 all-gather.10
  307.0 35.6 all-gather.12
  364.3 32.6 all-gather.14
  687.7 32.4 all-gather.16
where the time goes:
time: 1240 us; the launch traced here: 1220 us
  other arithmetic  675 us (54%)
  waiting for transfers between devices  223 us (18%)
  matrix products  145 us (12%)
  local copies, waits for them, and re-layouts  62.3 us (5%)
  starting transfers between devices  54.2 us (4%)
  blocking collectives  41.6 us (3%)
  between operations  21.2 us (2%)
    another operation x72, other arithmetic, factor_inverse(): lower_factor = jnp.linalg.cholesky(matrix)  309 us
    another operation x48, other arithmetic, factor_inverse(): jax.scipy.linalg.solve_triangular(lower_factor, identity, lower=True)  277 us
    all_gather x4, waiting for transfers between devices, group_gather(): gathered = lax.all_gather(pieces[:, None], 'front', axis=1, tiled=True)  139 us
    dot_general x90, matrix products, product(): jnp.dot(left, right, precision=lax.Precision.HIGHEST, preferred_element_t...  133 us
    ppermute x15, waiting for transfers between devices, partner_2(): return lax.ppermute(value, axis, pairs)  83.9 us
    ppermute x15, starting transfers between devices, partner_2(): return lax.ppermute(value, axis, pairs)  54 us
    all_gather x2, blocking collectives, group_gather(): gathered = lax.all_gather(pieces[:, None], 'front', axis=1, tiled=True)  41.6 us
    select_n x12, other arithmetic, join_pieces(): jnp.where(upper_bit == 0, jnp.concatenate([mine, theirs], axis_index), jn...  27.9 us
  transfers between devices with their start and end apart: 19, of which 16 were waited for; matrix products, arithmetic and copies ran while one was open for 4% of the time, Pallas kernels for 0%

commit v1 on v0

--- a/solution.py
+++ b/solution.py
@@ -1,6 +1,10 @@
+import functools
+
 import jax
 import jax.numpy as jnp
 from jax import lax
+from jax.experimental import pallas as pl
+from jax.experimental.pallas import tpu as pltpu
 from jax.sharding import PartitionSpec as P
 
 BLK = 128
@@ -17,36 +21,109 @@
     return jnp.dot(left, right, precision=lax.Precision.HIGHEST, preferred_element_type=jnp.float32)
 
 
-def factor_inverse(matrix):
-    order_size = matrix.shape[0]
-    if order_size <= 128 or order_size % 2 != 0:
-        lower_factor = jnp.linalg.cholesky(matrix)
-        identity = jnp.eye(order_size, dtype=jnp.float32)
-        inverse = jax.scipy.linalg.solve_triangular(lower_factor, identity, lower=True)
-        return (lower_factor, inverse)
-    half = order_size // 2
-    first_factor, first_inverse = factor_inverse(matrix[:half, :half])
-    coupling = product(matrix[half:, :half], first_inverse.T)
-    second_factor, second_inverse = factor_inverse(
-        matrix[half:, half:] - product(coupling, coupling.T)
-    )
-    corner = -product(second_inverse, product(coupling, first_inverse))
-    zeros_block = jnp.zeros((half, half), jnp.float32)
-    lower_factor = jnp.concatenate(
-        [
-            jnp.concatenate([first_factor, zeros_block], 1),
-            jnp.concatenate([coupling, second_factor], 1),
-        ],
-        0,
-    )
-    inverse = jnp.concatenate(
-        [
-            jnp.concatenate([first_inverse, zeros_block], 1),
-            jnp.concatenate([corner, second_inverse], 1),
-        ],
-        0,
-    )
-    return (lower_factor, inverse)
+SB = 16
+
+def split(x):
+    h = x.astype(jnp.bfloat16)
+    return h, (x - h.astype(jnp.float32)).astype(jnp.bfloat16)
+
+def dotb(a, b):
+    return jnp.dot(a, b, preferred_element_type=jnp.float32)
+
+def dott(a, b):
+    return lax.dot_general(a, b, (((1,), (1,)), ((), ())), preferred_element_type=jnp.float32)
+
+def substep(g_ref, u_ref, s):
+    base = s * SB
+    p = g_ref[base:base + SB, :]
+    cols = [jnp.broadcast_to(p[:, base + k:base + k + 1], (SB, 128)) for k in range(SB)]
+    pl_, pr_ = p[:, :128], p[:, 128:]
+    sub = lax.broadcasted_iota(jnp.int32, (SB, 128), 0)
+    ul = jnp.zeros((SB, 128), jnp.float32)
+    ur = jnp.zeros((SB, 128), jnp.float32)
+    for r in range(SB):
+        hit = sub == r
+        v = cols[r]
+        piv = jnp.broadcast_to(v[r:r + 1], (SB, 128))
+        rs = lax.rsqrt(piv)
+        inv = rs * rs
+        rl = jnp.broadcast_to(pl_[r:r + 1], (SB, 128))
+        rr = jnp.broadcast_to(pr_[r:r + 1], (SB, 128))
+        ul = jnp.where(hit, rl * rs, ul)
+        ur = jnp.where(hit, rr * rs, ur)
+        vi = jnp.where(hit, 0.0, v * inv)
+        for k in range(r + 1, SB):
+            c = jnp.broadcast_to(cols[k][r:r + 1], (SB, 128))
+            cols[k] = jnp.where(hit, c * inv, cols[k] - vi * c)
+        pl_ = jnp.where(hit, rl * inv, pl_ - vi * rl)
+        pr_ = jnp.where(hit, rr * inv, pr_ - vi * rr)
+    u_ref[base:base + SB, :128] = ul
+    u_ref[base:base + SB, 128:] = ur
+    if s < 128 // SB - 1:
+        lo = base + SB
+        R = jnp.concatenate([pl_, pr_], 1)
+        rh, rlo = split(R)
+        parts = []
+        def pad(x):
+            z = []
+            if base: z.append(jnp.zeros((base, 256), jnp.bfloat16))
+            z.append(x)
+            if 128 - lo: z.append(jnp.zeros((128 - lo, 256), jnp.bfloat16))
+            return jnp.concatenate(z, 0)
+        d = g_ref[lo:, :128]
+        dh, dl = split(d)
+        upd = dotb(jnp.concatenate([dh, dl], 1), jnp.concatenate([pad(rh), pad(rh)], 0)) + dotb(dh, pad(rlo))
+        g_ref[lo:, :] = g_ref[lo:, :] - upd
+
+def kernel(m, a_ref, b_ref, l_ref, x_ref, xh, xl, col, g_ref, u_ref):
+    n = 8
+    lane = lax.broadcasted_iota(jnp.int32, (128, 128), 1)
+    row = lax.broadcasted_iota(jnp.int32, (128, 128), 0)
+    def step(k, _):
+        for kk in range(n):
+            @pl.when(k == kk)
+            def _():
+                rows = 1024 - kk * 128
+                c = jnp.concatenate([a_ref[kk * 128:, kk * 128:(kk + 1) * 128], b_ref[:, kk * 128:(kk + 1) * 128]], 0)
+                if kk:
+                    K = kk * 128
+                    rh, rl = xh[kk * 128:(kk + 1) * 128, :K], xl[kk * 128:(kk + 1) * 128, :K]
+                    c = c - (dott(xh[kk * 128:, :K], rh) + (dott(xh[kk * 128:, :K], rl) + dott(xl[kk * 128:, :K], rh)))
+                g_ref[:, :128] = c[:128]
+                col[kk * 128 + 128:, :] = c[128:]
+        g_ref[:, 128:] = jnp.where(lane == row, 1.0, 0.0)
+        for s in range(128 // SB):
+            substep(g_ref, u_ref, s)
+        k128 = pl.multiple_of(k * 128, 128)
+        l_ref[pl.ds(k128, 128), pl.ds(k128, 128)] = jnp.where(lane <= row, u_ref[:, :128].T, 0.0)
+        wh, wl = split(u_ref[:, 128:])
+        for kk in range(n):
+            @pl.when(k == kk)
+            def _():
+                ch, cl = split(col[kk * 128 + 128:, :])
+                x = dott(ch, wh) + (dott(ch, wl) + dott(cl, wh))
+                if kk < n - 1:
+                    l_ref[kk * 128 + 128:, kk * 128:(kk + 1) * 128] = x[:1024 - kk * 128 - 128]
+                    l_ref[:kk * 128 + 128, (kk + 1) * 128:(kk + 2) * 128] = jnp.zeros((kk * 128 + 128, 128), jnp.float32)
+                x_ref[:, kk * 128:(kk + 1) * 128] = x[1024 - kk * 128 - 128:]
+                h, l = split(x)
+                xh[kk * 128 + 128:, kk * 128:(kk + 1) * 128] = h
+                xl[kk * 128 + 128:, kk * 128:(kk + 1) * 128] = l
+        return 0
+    lax.fori_loop(0, n, step, 0)
+
+def factor_panel(a, b):
+    m = b.shape[0]
+    vm = pl.BlockSpec(memory_space=pltpu.VMEM)
+    return pl.pallas_call(
+        functools.partial(kernel, m),
+        out_shape=(jax.ShapeDtypeStruct((1024, 1024), jnp.float32), jax.ShapeDtypeStruct((m, 1024), jnp.float32)),
+        in_specs=[vm, vm], out_specs=(vm, vm),
+        scratch_shapes=[pltpu.VMEM((1024 + m, 1024), jnp.bfloat16), pltpu.VMEM((1024 + m, 1024), jnp.bfloat16),
+                        pltpu.VMEM((1024 + m, 128), jnp.float32), pltpu.VMEM((128, 256), jnp.float32), pltpu.VMEM((128, 256), jnp.float32)],
+        compiler_params=pltpu.CompilerParams(vmem_limit_bytes=60 * 2**20),
+        name="factor_panel",
+    )(a, b)
 
 
 def reversed_bits(number, bit_count):
@@ -137,8 +214,7 @@
         piece_index = reversed_bits(leaf_index & 2**height - 1, height)
         update_pivot = update_slab[:, :, :pivot_size]
         whole_pivot = group_gather(pivot_slab, height).reshape(pivot_size, pivot_size)
-        lower_factor, factor_inv = factor_inverse(whole_pivot)
-        own_panel = product(update_pivot.reshape(-1, pivot_size), factor_inv.T)
+        lower_factor, own_panel = factor_panel(whole_pivot, update_pivot.reshape(-1, pivot_size))
         all_panel = group_gather(
             own_panel.reshape(local_count, piece_rows, pivot_size), height
         ).reshape(pivot_size, pivot_size)

time: 1240 us -> 541 us (0.44)
  other arithmetic: 675 us -> 36.9 us
  matrix products: 145 us -> 12.3 us
  Pallas kernels: 0 us -> 119 us
  local copies, waits for them, and re-layouts: 62.3 us -> 5.53 us
  waiting for transfers between devices: 223 us -> 242 us
    another operation x120 -> x0, other arithmetic: 586 us -> none  [the longest x72 309 us: factor_inverse(): lower_factor = jnp.linalg.cholesky(matrix)]
    dot_general x90 -> x3, matrix products: 133 us -> 12.3 us  [product(): jnp.dot(left, right, precision=lax.Precision.HIGHEST, preferred_element_t...]
    pallas_call x0 -> x3, Pallas kernels: none -> 119 us  [factor_panel(): pl.pallas_call(functools.partial(kernel, m), out_shape=(jax.ShapeDtypeStr...]
    concatenate x21 -> x0, other arithmetic: 28.4 us -> none  [the longest x12 21.2 us: factor_inverse(): jnp.concatenate([jnp.concatenate([first_factor, zeros_block], 1), jnp.con...]
    ppermute x15, waiting for transfers between devices: 83.9 us -> 103 us  [partner_2(): return lax.ppermute(value, axis, pairs)]
    unnamed x231 -> x23, local copies, waits for them, and re-layouts: 17.8 us -> 0.32 us
    slice x27 -> x0, local copies, waits for them, and re-layouts: 15.3 us -> none  [the longest x6 8.8 us: factor_inverse(): matrix[half:, half:] - product(coupling, coupling.T)]
    dot_general x21 -> x0, local copies, waits for them, and re-layouts: 14.8 us -> none  [product(): jnp.dot(left, right, precision=lax.Precision.HIGHEST, preferred_element_t...]
  transfers between devices with their start and end apart: 19 -> 19, of which waited for: 16 -> 17; matrix products, arithmetic and copies ran while one was open for 4% -> 3% of each run, Pallas kernels for 0% -> 0%
where the time goes in v1:
time: 541 us; the launch traced here: 533 us
  waiting for transfers between devices  242 us (45%)
  Pallas kernels  119 us (22%)
  starting transfers between devices  58.8 us (11%)
  blocking collectives  39.2 us (7%)
  other arithmetic  36.9 us (7%)
  between operations  18.6 us (3%)
  matrix products  12.3 us (2%)
  local copies, waits for them, and re-layouts  5.53 us (1%)
    all_gather x4, waiting for transfers between devices, group_gather(): gathered = lax.all_gather(pieces[:, None], 'front', axis=1, tiled=True)  139 us
    pallas_call x3, Pallas kernels, factor_panel(): pl.pallas_call(functools.partial(kernel, m), out_shape=(jax.ShapeDtypeStr...  119 us
    ppermute x15, waiting for transfers between devices, partner_2(): return lax.ppermute(value, axis, pairs)  103 us
    ppermute x15, starting transfers between devices, partner_2(): return lax.ppermute(value, axis, pairs)  58.7 us
    all_gather x2, blocking collectives, group_gather(): gathered = lax.all_gather(pieces[:, None], 'front', axis=1, tiled=True)  39.2 us
    select_n x12, other arithmetic, join_pieces(): jnp.where(upper_bit == 0, jnp.concatenate([mine, theirs], axis_index), jn...  23.7 us
    dot_general x3, matrix products, product(): jnp.dot(left, right, precision=lax.Precision.HIGHEST, preferred_element_t...  12.3 us
  transfers between devices with their start and end apart: 19, of which 17 were waited for; matrix products, arithmetic and copies ran while one was open for 3% of the time, Pallas kernels for 0%

profile of v1, /device:TPU:1, one launch (start us, length us, event | category | flops | bytes accessed | tf_op | source)
XLA Modules:
  0.0 532.8 jit_solution(12157570404904428514)
XLA Ops:
  7.2 1.1 select_bitcast_fusion
  8.3 3.3 collective-permute-start
  12.7 0.7 broadcast_multiply_fusion
  15.1 0.9 fusion.4
  16.0 38.2 %all-gather.11.cloned.1.call-done = f32[8,64,1024]{2,1,0:T(8,128)} async-done(((f32[1,64,1024]{2,1,0:T(8,128)}), f32[8,64,1024]{2,1,0:T(8,128)}) %all-gather.11.cloned.1.call-update) | async-done | bytes 2097168 | tf_op jit(solution)/shard_map/all_gather | solution.py:146
  54.2 4.4 collective-permute-start.1
  58.6 0.7 multiply_add_fusion
  59.3 0.7 slice_bitcast_fusion.1.b_ref
  60.1 2.6 collective-permute-done.1
  62.6 5.2 maximum_select_fusion
  67.8 39.6 %factor_panel.3 = (f32[1024,1024]{1,0:T(8,128)}, f32[64,1024]{1,0:T(8,128)}) custom-call(f32[1024,1024]{1,0:T(8,128)} %bitcast.162, f32[64,1024]{1,0:T(8,128)} %slice_bitcast_fusion.1.b_ref), custom_call_target="tpu_custom_call" | custom-call | tf_op jit(solution)/shard_map/factor_panel/pallas_call | solution.py:118
  107.5 35.7 %all-gather.13.cloned.1.call-done = f32[512,1024]{1,0:T(8,128)} async-done(((f32[64,1024]{1,0:T(8,128)}), f32[512,1024]{1,0:T(8,128)}) %all-gather.13.cloned.1.call-update) | async-done | bytes 2097168 | tf_op jit(solution)/shard_map/all_gather | solution.py:146
  143.3 4.9 collective-permute-start.2
  148.1 0.7 compare_convert_fusion.1
  150.8 1.4 collective-permute-done.2
  152.1 2.9 maximum_select_fusion.1
  155.1 4.2 fusion
  159.5 1.3 collective-permute-start.3
  161.4 2.8 collective-permute-done.3
  164.5 0.7 fusion.7
  165.3 32.8 %all-gather.15.cloned.1.call-done = f32[8,32,1024]{2,1,0:T(8,128)} async-done(((f32[1,32,1024]{2,1,0:T(8,128)}), f32[8,32,1024]{2,1,0:T(8,128)}) %all-gather.15.cloned.1.call-update) | async-done | bytes 1048592 | tf_op jit(solution)/shard_map/all_gather | solution.py:146
  198.1 1.2 collective-permute-start.4
  199.3 17.9 %collective-permute-done.4 = f32[1,8,32,1024]{3,2,1,0:T(8,128)S(1)} collective-permute-done((f32[1,8,32,1024]{3,2,1,0:T(8,128)}, f32[1,8,32,1024]{3,2,1,0:T(8,128)S(1)}, u32[]{:S(2)}, u32[]{:S(2)}) %collective-permute-start.4) | collective-permute-done | bytes 1048608 | tf_op jit(solution)/shard_map/ppermute | solution.py:17
  217.2 2.0 maximum_select_fusion.6
  219.2 7.0 %collective-permute-start.5 = (f32[1,8,64,1024]{3,2,1,0:T(8,128)S(1)}, f32[1,8,64,1024]{3,2,1,0:T(8,128)S(1)}, u32[]{:S(2)}, u32[]{:S(2)}) collective-permute-start(f32[1,8,64,1024]{3,2,1,0:T(8,128)S(1)} %maximum_select_fusion.6), channel_id=1, source_target_pairs={{0,8},{8,0},{16,24},{24,16},{32,40},{40,32},{48,56},{56,48},{64,72... | collective-permute-start | bytes 6291464 | tf_op jit(solution)/shard_map/ppermute | solution.py:17
  226.2 0.7 multiply_add_fusion.1
  226.9 0.7 slice_bitcast_fusion.3.b_ref
  227.5 2.4 collective-permute-done.5
  230.0 2.5 maximum_select_fusion.2
  232.4 39.4 %factor_panel.4 = (f32[1024,1024]{1,0:T(8,128)}, f32[32,1024]{1,0:T(8,128)}) custom-call(f32[1024,1024]{1,0:T(8,128)} %bitcast.163, f32[32,1024]{1,0:T(8,128)} %slice_bitcast_fusion.3.b_ref), custom_call_target="tpu_custom_call" | custom-call | tf_op jit(solution)/shard_map/factor_panel/pallas_call | solution.py:118
  271.8 32.6 %all-gather.17.cloned.1.call-done = f32[256,1024]{1,0:T(8,128)} async-done(((f32[32,1024]{1,0:T(8,128)}), f32[256,1024]{1,0:T(8,128)}) %all-gather.17.cloned.1.call-update) | async-done | bytes 1048592 | tf_op jit(solution)/shard_map/all_gather | solution.py:146
  304.5 1.2 collective-permute-start.6
  305.6 17.9 %collective-permute-done.6 = f32[1,8,32,1024]{3,2,1,0:T(8,128)S(1)} collective-permute-done((f32[1,8,32,1024]{3,2,1,0:T(8,128)}, f32[1,8,32,1024]{3,2,1,0:T(8,128)S(1)}, u32[]{:S(2)}, u32[]{:S(2)}) %collective-permute-start.6) | collective-permute-done | bytes 1048608 | tf_op jit(solution)/shard_map/ppermute | solution.py:17
  323.5 1.9 maximum_select_fusion.7
  325.5 7.0 %collective-permute-start.7 = (f32[1,8,64,1024]{3,2,1,0:T(8,128)S(1)}, f32[1,8,64,1024]{3,2,1,0:T(8,128)}, u32[]{:S(2)}, u32[]{:S(2)}) collective-permute-start(f32[1,8,64,1024]{3,2,1,0:T(8,128)S(1)} %maximum_select_fusion.7), channel_id=1, source_target_pairs={{0,8},{8,0},{16,24},{24,16},{32,40},{40,32},{48,56},{56,48},{64,72... | collective-permute-start | bytes 6291464 | tf_op jit(solution)/shard_map/ppermute | solution.py:17
  332.5 0.7 compare_convert_fusion
  335.1 1.3 collective-permute-done.7
  336.4 2.9 maximum_select_fusion.3
  339.3 3.9 fusion.1
  343.5 2.8 collective-permute-start.8
  346.9 1.3 collective-permute-done.8
  348.4 19.8 %all-gather.4 = f32[8,16,1024]{2,1,0:T(8,128)S(1)} all-gather(f32[1,16,1024]{2,1,0:T(8,128)S(1)} %get-tuple-element.77), channel_id=6, replica_groups=mesh['leaf'=32,'front'=8] {'front'}, dimensions={0}, use_global_device_ids=true | all-gather | bytes 589824 | tf_op jit(solution)/shard_map/all_gather | solution.py:146
  368.2 2.7 collective-permute-start.9
  370.9 6.8 %collective-permute-done.9 = f32[1,8,16,1024]{3,2,1,0:T(8,128)S(1)} collective-permute-done((f32[1,8,16,1024]{3,2,1,0:T(8,128)S(1)}, f32[1,8,16,1024]{3,2,1,0:T(8,128)S(1)}, u32[]{:S(2)}, u32[]{:S(2)}) %collective-permute-start.9) | collective-permute-done | bytes 524320 | tf_op jit(solution)/shard_map/ppermute | solution.py:17
  377.9 1.3 collective-permute-start.10
  379.3 21.0 %collective-permute-done.10 = f32[1,8,32,1024]{3,2,1,0:T(8,128)S(1)} collective-permute-done((f32[1,8,32,1024]{3,2,1,0:T(8,128)S(1)}, f32[1,8,32,1024]{3,2,1,0:T(8,128)S(1)}, u32[]{:S(2)}, u32[]{:S(2)}) %collective-permute-start.10) | collective-permute-done | bytes 1048608 | tf_op jit(solution)/shard_map/ppermute | solution.py:17
  400.6 8.5 %collective-permute-start.11 = (f32[1,8,64,1024]{3,2,1,0:T(8,128)S(1)}, f32[1,8,64,1024]{3,2,1,0:T(8,128)S(1)}, u32[]{:S(2)}, u32[]{:S(2)}) collective-permute-start(f32[1,8,64,1024]{3,2,1,0:T(8,128)S(1)} %maximum_select_fusion.8), channel_id=1, source_target_pairs={{0,8},{8,0},{16,24},{24,16},{32,40},{40,32},{48,56},{56,48},{64,72... | collective-permute-start | bytes 6291464 | tf_op jit(solution)/shard_map/ppermute | solution.py:17
  410.4 2.5 collective-permute-done.11
  412.9 2.4 maximum_select_fusion.4
  415.2 40.1 %factor_panel.5 = (f32[1024,1024]{1,0:T(8,128)}, f32[16,1024]{1,0:T(8,128)}) custom-call(f32[1024,1024]{1,0:T(8,128)} %bitcast.164, f32[16,1024]{1,0:T(8,128)} %slice_bitcast_fusion.5.b_ref), custom_call_target="tpu_custom_call" | custom-call | tf_op jit(solution)/shard_map/factor_panel/pallas_call | solution.py:118
  455.4 19.4 %all-gather.5 = f32[128,1024]{1,0:T(8,128)S(1)} all-gather(f32[16,1024]{1,0:T(8,128)} %get-tuple-element.51), channel_id=7, replica_groups=mesh['leaf'=32,'front'=8] {'front'}, dimensions={0}, use_global_device_ids=true | all-gather | bytes 589824 | tf_op jit(solution)/shard_map/all_gather | solution.py:146
  474.8 1.8 collective-permute-start.12
  476.6 7.8 %collective-permute-done.12 = f32[1,8,16,1024]{3,2,1,0:T(8,128)S(1)} collective-permute-done((f32[1,8,16,1024]{3,2,1,0:T(8,128)S(1)}, f32[1,8,16,1024]{3,2,1,0:T(8,128)S(1)}, u32[]{:S(2)}, u32[]{:S(2)}) %collective-permute-start.12) | collective-permute-done | bytes 524320 | tf_op jit(solution)/shard_map/ppermute | solution.py:17
  484.5 1.3 collective-permute-start.13
  485.9 17.2 %collective-permute-done.13 = f32[1,8,32,1024]{3,2,1,0:T(8,128)S(1)} collective-permute-done((f32[1,8,32,1024]{3,2,1,0:T(8,128)S(1)}, f32[1,8,32,1024]{3,2,1,0:T(8,128)S(1)}, u32[]{:S(2)}, u32[]{:S(2)}) %collective-permute-start.13) | collective-permute-done | bytes 1048608 | tf_op jit(solution)/shard_map/ppermute | solution.py:17
  503.3 10.2 %collective-permute-start.14 = (f32[1,8,64,1024]{3,2,1,0:T(8,128)S(1)}, f32[1,8,64,1024]{3,2,1,0:T(8,128)}, u32[]{:S(2)}, u32[]{:S(2)}) collective-permute-start(f32[1,8,64,1024]{3,2,1,0:T(8,128)S(1)} %maximum_select_fusion.9), channel_id=1, source_target_pairs={{0,8},{8,0},{16,24},{24,16},{32,40},{40,32},{48,56},{56,48},{64,72... | collective-permute-start | bytes 6291464 | tf_op jit(solution)/shard_map/ppermute | solution.py:17
  513.5 1.0 dynamic-slice_bitcast_fusion
  514.5 0.8 pad_maximum_fusion.2
  515.3 0.9 dynamic-slice_bitcast_fusion.1
  516.3 0.7 pad_maximum_fusion.5
  517.0 0.9 dynamic-slice_bitcast_fusion.2
  517.9 0.7 pad_maximum_fusion.8
  518.6 3.0 maximum_select_fusion.5
  521.6 4.2 convolution_subtract_fusion.2
  (75 shorter events, 7.3 us)
Async XLA Ops:
  7.2 4.5 copy-start
  7.2 47.1 %all-gather.11.cloned.1.call-start = ((), (), s32[]{:S(2)}) async-start(), calls=%async_computation | async-start | bytes 2359296 | tf_op jit(solution)/shard_map/all_gather | solution.py:146
  8.3 6.7 %copy-start.5 = (f32[128,1024]{1,0:T(8,128)S(1)}, f32[128,1024]{1,0:T(8,128)}, u32[]{:S(2)}) copy-start(f32[128,1024]{1,0:T(8,128)} %param.14) | copy-start | bytes 1572868
  8.3 6.4 %collective-permute-start = (f32[1,64,1024]{2,1,0:T(8,128)S(1)}, f32[1,64,1024]{2,1,0:T(8,128)S(1)}, u32[]{:S(2)}, u32[]{:S(2)}) collective-permute-start(f32[1,64,1024]{2,1,0:T(8,128)S(1)} %get-tuple-element.67), channel_id=1, source_target_pairs={{0,8},{8,0},{16,24},{24,16},{32,40},{40,32},{48,56},{56,48},{64,72... | collective-permute-start | bytes 786440 | tf_op jit(solution)/shard_map/ppermute | solution.py:17
  16.0 127.3 %all-gather.13.cloned.1.call-start = ((), (), s32[]{:S(2)}) async-start(), calls=%async_computation.1 | async-start | bytes 2359296 | tf_op jit(solution)/shard_map/all_gather | solution.py:146
  54.2 8.4 %collective-permute-start.1 = (f32[1,8,64,1024]{3,2,1,0:T(8,128)}, f32[1,8,64,1024]{3,2,1,0:T(8,128)S(1)}, u32[]{:S(2)}, u32[]{:S(2)}) collective-permute-start(f32[1,8,64,1024]{3,2,1,0:T(8,128)} %bitcast.177), channel_id=1, source_target_pairs={{0,8},{8,0},{16,24},{24,16},{32,40},{40,32},{48,56},{56,48},{64,72... | collective-permute-start | bytes 6291464 | tf_op jit(solution)/shard_map/ppermute | solution.py:17
  107.5 90.7 %all-gather.15.cloned.1.call-start = ((), (), s32[]{:S(2)}) async-start(), calls=%async_computation.2 | async-start | bytes 1179648 | tf_op jit(solution)/shard_map/all_gather | solution.py:146
  143.3 8.9 %collective-permute-start.2 = (f32[1,8,64,1024]{3,2,1,0:T(8,128)}, f32[1,8,64,1024]{3,2,1,0:T(8,128)S(1)}, u32[]{:S(2)}, u32[]{:S(2)}) collective-permute-start(f32[1,8,64,1024]{3,2,1,0:T(8,128)} %bitcast.175), channel_id=1, source_target_pairs={{0,8},{8,0},{16,24},{24,16},{32,40},{40,32},{48,56},{56,48},{64,72... | collective-permute-start | bytes 6291464 | tf_op jit(solution)/shard_map/ppermute | solution.py:17
  150.8 4.3 copy-start.2
  155.1 9.4 %copy-start.6 = (f32[64,1024]{1,0:T(8,128)S(1)}, f32[64,1024]{1,0:T(8,128)}, u32[]{:S(2)}) copy-start(f32[64,1024]{1,0:T(8,128)} %param.15) | copy-start | bytes 786436
  159.5 4.8 collective-permute-start.3
  165.3 139.2 %all-gather.17.cloned.1.call-start = ((), (), s32[]{:S(2)}) async-start(), calls=%async_computation.3 | async-start | bytes 1179648 | tf_op jit(solution)/shard_map/all_gather | solution.py:146
  198.1 19.1 %collective-permute-start.4 = (f32[1,8,32,1024]{3,2,1,0:T(8,128)}, f32[1,8,32,1024]{3,2,1,0:T(8,128)S(1)}, u32[]{:S(2)}, u32[]{:S(2)}) collective-permute-start(f32[1,8,32,1024]{3,2,1,0:T(8,128)} %bitcast.179), channel_id=1, source_target_pairs={{0,16},{8,24},{16,0},{24,8},{32,48},{40,56},{48,32},{56,40},{64,80... | collective-permute-start | bytes 3145736 | tf_op jit(solution)/shard_map/ppermute | solution.py:17
  219.2 10.7 %collective-permute-start.5 = (f32[1,8,64,1024]{3,2,1,0:T(8,128)S(1)}, f32[1,8,64,1024]{3,2,1,0:T(8,128)S(1)}, u32[]{:S(2)}, u32[]{:S(2)}) collective-permute-start(f32[1,8,64,1024]{3,2,1,0:T(8,128)S(1)} %maximum_select_fusion.6), channel_id=1, source_target_pairs={{0,8},{8,0},{16,24},{24,16},{32,40},{40,32},{48,56},{56,48},{64,72... | collective-permute-start | bytes 6291464 | tf_op jit(solution)/shard_map/ppermute | solution.py:17
  304.5 19.1 %collective-permute-start.6 = (f32[1,8,32,1024]{3,2,1,0:T(8,128)}, f32[1,8,32,1024]{3,2,1,0:T(8,128)S(1)}, u32[]{:S(2)}, u32[]{:S(2)}) collective-permute-start(f32[1,8,32,1024]{3,2,1,0:T(8,128)} %bitcast.181), channel_id=1, source_target_pairs={{0,16},{8,24},{16,0},{24,8},{32,48},{40,56},{48,32},{56,40},{64,80... | collective-permute-start | bytes 3145736 | tf_op jit(solution)/shard_map/ppermute | solution.py:17
  325.5 10.9 %collective-permute-start.7 = (f32[1,8,64,1024]{3,2,1,0:T(8,128)S(1)}, f32[1,8,64,1024]{3,2,1,0:T(8,128)}, u32[]{:S(2)}, u32[]{:S(2)}) collective-permute-start(f32[1,8,64,1024]{3,2,1,0:T(8,128)S(1)} %maximum_select_fusion.7), channel_id=1, source_target_pairs={{0,8},{8,0},{16,24},{24,16},{32,40},{40,32},{48,56},{56,48},{64,72... | collective-permute-start | bytes 6291464 | tf_op jit(solution)/shard_map/ppermute | solution.py:17
  335.1 4.3 copy-start.3
  339.3 9.0 %copy-start.7 = (f32[32,1024]{1,0:T(8,128)S(1)}, f32[32,1024]{1,0:T(8,128)}, u32[]{:S(2)}) copy-start(f32[32,1024]{1,0:T(8,128)} %param.16) | copy-start | bytes 393220
  343.5 4.7 collective-permute-start.8
  368.2 9.5 %collective-permute-start.9 = (f32[1,8,16,1024]{3,2,1,0:T(8,128)S(1)}, f32[1,8,16,1024]{3,2,1,0:T(8,128)S(1)}, u32[]{:S(2)}, u32[]{:S(2)}) collective-permute-start(f32[1,8,16,1024]{3,2,1,0:T(8,128)S(1)} %bitcast.168), channel_id=1, source_target_pairs={{0,32},{8,40},{16,48},{24,56},{32,0},{40,8},{48,16},{56,24},{64,96... | collective-permute-start | bytes 1572872 | tf_op jit(solution)/shard_map/ppermute | solution.py:17
  377.9 22.4 %collective-permute-start.10 = (f32[1,8,32,1024]{3,2,1,0:T(8,128)S(1)}, f32[1,8,32,1024]{3,2,1,0:T(8,128)S(1)}, u32[]{:S(2)}, u32[]{:S(2)}) collective-permute-start(f32[1,8,32,1024]{3,2,1,0:T(8,128)S(1)} %maximum_select_fusion.11), channel_id=1, source_target_pairs={{0,16},{8,24},{16,0},{24,8},{32,48},{40,56},{48,32},{56,40},{64,80... | collective-permute-start | bytes 3145736 | tf_op jit(solution)/shard_map/ppermute | solution.py:17
  400.6 12.3 %collective-permute-start.11 = (f32[1,8,64,1024]{3,2,1,0:T(8,128)S(1)}, f32[1,8,64,1024]{3,2,1,0:T(8,128)S(1)}, u32[]{:S(2)}, u32[]{:S(2)}) collective-permute-start(f32[1,8,64,1024]{3,2,1,0:T(8,128)S(1)} %maximum_select_fusion.8), channel_id=1, source_target_pairs={{0,8},{8,0},{16,24},{24,16},{32,40},{40,32},{48,56},{56,48},{64,72... | collective-permute-start | bytes 6291464 | tf_op jit(solution)/shard_map/ppermute | solution.py:17
  474.8 9.5 %collective-permute-start.12 = (f32[1,8,16,1024]{3,2,1,0:T(8,128)S(1)}, f32[1,8,16,1024]{3,2,1,0:T(8,128)S(1)}, u32[]{:S(2)}, u32[]{:S(2)}) collective-permute-start(f32[1,8,16,1024]{3,2,1,0:T(8,128)S(1)} %bitcast.170), channel_id=1, source_target_pairs={{0,32},{8,40},{16,48},{24,56},{32,0},{40,8},{48,16},{56,24},{64,96... | collective-permute-start | bytes 1572872 | tf_op jit(solution)/shard_map/ppermute | solution.py:17
  484.5 18.5 %collective-permute-start.13 = (f32[1,8,32,1024]{3,2,1,0:T(8,128)S(1)}, f32[1,8,32,1024]{3,2,1,0:T(8,128)S(1)}, u32[]{:S(2)}, u32[]{:S(2)}) collective-permute-start(f32[1,8,32,1024]{3,2,1,0:T(8,128)S(1)} %maximum_select_fusion.13), channel_id=1, source_target_pairs={{0,16},{8,24},{16,0},{24,8},{32,48},{40,56},{48,32},{56,40},{64,80... | collective-permute-start | bytes 3145736 | tf_op jit(solution)/shard_map/ppermute | solution.py:17
  485.7 32.2 %copy-start.4 = (f32[16,1024]{1,0:T(8,128)S(1)}, f32[16,1024]{1,0:T(8,128)}, u32[]{:S(2)}) copy-start(f32[16,1024]{1,0:T(8,128)} %get-tuple-element.51) | copy-start | bytes 196612
  503.3 15.3 %collective-permute-start.14 = (f32[1,8,64,1024]{3,2,1,0:T(8,128)S(1)}, f32[1,8,64,1024]{3,2,1,0:T(8,128)}, u32[]{:S(2)}, u32[]{:S(2)}) collective-permute-start(f32[1,8,64,1024]{3,2,1,0:T(8,128)S(1)} %maximum_select_fusion.9), channel_id=1, source_target_pairs={{0,8},{8,0},{16,24},{24,16},{32,40},{40,32},{48,56},{56,48},{64,72... | collective-permute-start | bytes 6291464 | tf_op jit(solution)/shard_map/ppermute | solution.py:17
  518.6 7.2 %copy-start.1 = (s32[16,2,8]{0,2,1:T(8,128)S(1)}, s32[16,2,8]{0,2,1:T(8,128)}, u32[]{:S(2)}) copy-start(s32[16,2,8]{0,2,1:T(8,128)} %param.17) | copy-start | bytes 3076
Sparse Core Ops, SparseCore 0:
  16.1 38.1 all-gather.10
  107.6 35.6 all-gather.12
  165.4 32.6 all-gather.14
  271.9 32.4 all-gather.16

commit v2 on v1

--- a/solution.py
+++ b/solution.py
@@ -8,19 +8,6 @@
 from jax.sharding import PartitionSpec as P
 
 BLK = 128
-PIVOT_BLOCKS = 8
-
-
-def partner_2(value, axis, stride):
-    mask = 2**stride
-    pairs = [(source, source ^ mask) for source in range(lax.axis_size(axis))]
-    return lax.ppermute(value, axis, pairs)
-
-
-def product(left, right):
-    return jnp.dot(left, right, precision=lax.Precision.HIGHEST, preferred_element_type=jnp.float32)
-
-
 SB = 16
 
 def split(x):
@@ -126,42 +113,234 @@
     )(a, b)
 
 
-def reversed_bits(number, bit_count):
-    result = jnp.zeros((), jnp.int32)
-    for bit_index in range(bit_count):
-        result = result + (number >> bit_index & 1) * (1 << bit_count - 1 - bit_index)
-    return result
-
-
-def join_pieces(mine, theirs, bit_index, axis_index):
-    upper_bit = lax.axis_index("leaf") >> bit_index & 1
-    return jnp.where(
-        upper_bit == 0,
-        jnp.concatenate([mine, theirs], axis_index),
-        jnp.concatenate([theirs, mine], axis_index),
+MESH = pl.DeviceIdType.MESH
+NB = 8
+
+
+class Place:
+    def __init__(self, height):
+        self.height = height
+        self.m = BLK >> height
+        self.leaf = lax.axis_index("leaf")
+        self.f = lax.axis_index("front")
+        self.core = lax.rem(self.leaf, 2)
+        member = lax.rem(self.leaf, 2**height)
+        piece = 0
+        for bit in range(height):
+            piece = piece + lax.rem(member // 2**bit, 2) * 2 ** (height - 1 - bit)
+        self.piece = piece
+        self.rest = lax.rem(piece, 2 ** (height - 1))
+        self.peers = [self.flip(2 * d) for d in range(1, 2 ** (height - 1))]
+        self.mate = self.flip(1)
+        self.right = (self.leaf, lax.rem(self.f + 1, NB))
+        self.left = (self.leaf, lax.rem(self.f + NB - 1, NB))
+
+    def flip(self, mask):
+        other = self.leaf
+        bit = 1
+        while bit <= mask:
+            if mask & bit:
+                other = other + bit * (1 - 2 * lax.rem(self.leaf // bit, 2))
+            bit *= 2
+        return (other, self.f)
+
+    def greet(self):
+        barrier = pltpu.get_barrier_semaphore()
+        others = [self.left, self.right, self.mate] + self.peers
+        for other in others:
+            pl.semaphore_signal(barrier, inc=1, device_id=other, device_id_type=MESH)
+        pl.semaphore_wait(barrier, len(others))
+
+
+def guarded(cond, body):
+    if cond is None:
+        body()
+    else:
+        pl.when(cond)(body)
+
+
+def remote(src, dst, send, recv, device):
+    return pltpu.make_async_remote_copy(
+        src_ref=src, dst_ref=dst, send_sem=send, recv_sem=recv, device_id=device, device_id_type=MESH
     )
 
 
-def group_gather(pieces, height):
-    gathered = lax.all_gather(pieces[:, None], "front", axis=1, tiled=True)
-    for bit_index in reversed(range(height)):
-        partner = partner_2(gathered, "leaf", bit_index)
-        gathered = join_pieces(gathered, partner, bit_index, 2)
-    return gathered
-
-
-def spread_columns(rows_in, upper_mask):
-    blocks = rows_in.reshape(rows_in.shape[0], rows_in.shape[1], upper_mask.shape[0], -1)
-    to_pivot = blocks * (1.0 - upper_mask)[None, None, :, None]
-    to_update = blocks * upper_mask[None, None, :, None]
-    return jnp.concatenate([to_pivot, to_update], axis=2).reshape(
-        rows_in.shape[0], rows_in.shape[1], -1
-    )
-
-
-def own_rows(whole, front_index, piece_index, piece_rows):
-    chosen = lax.dynamic_index_in_dim(whole, front_index, 1, keepdims=False)
-    return lax.dynamic_slice_in_dim(chosen, piece_index * piece_rows, piece_rows, 1)
+GATHER_SEMS = [
+    pltpu.SemaphoreType.DMA((3, NB)),
+    pltpu.SemaphoreType.DMA((3, NB)),
+    pltpu.SemaphoreType.DMA((2, 4, NB)),
+    pltpu.SemaphoreType.DMA((2, 4, NB)),
+    pltpu.SemaphoreType.DMA((NB, NB)),
+    pltpu.SemaphoreType.DMA((NB, NB)),
+]
+
+
+def gather(place, whole, sems, lower):
+    xs, xr, zs, zr, cs, cr = sems
+    m = place.m
+
+    def need(origin, q):
+        return (origin >= q) if lower and q else None
+
+    def slab(origin, q, core):
+        return whole.at[origin, pl.ds(pl.multiple_of(core * 64, 64), 64), pl.ds(q * BLK, BLK)]
+
+    def piece(index, q):
+        rows = pl.ds(pl.multiple_of(index * m, m), m)
+        return whole.at[place.f, rows, pl.ds(q * BLK, BLK)]
+
+    def peer_copy(d, q):
+        mine = piece(place.piece, q)
+        return remote(mine, mine, xs.at[d, q], xr.at[d, q], place.peers[d])
+
+    def ring_copy(way, hop, q):
+        origin = lax.rem(place.f + ((NB - hop) if way == 0 else hop), NB)
+        mine = slab(origin, q, place.core)
+        return origin, remote(mine, mine, zs.at[way, hop, q], zr.at[way, hop, q], (place.right, place.left)[way])
+
+    def arrival(way, hop, q):
+        origin = lax.rem(place.f + ((NB - hop) if way == 0 else hop), NB)
+        mine = slab(origin, q, place.core)
+        return origin, remote(mine, mine, zs.at[way, hop - 1, q], zr.at[way, hop - 1, q], (place.right, place.left)[way])
+
+    def mate_copy(origin, slot, q):
+        mine = slab(origin, q, place.core)
+        return remote(mine, mine, cs.at[slot, q], cr.at[slot, q], place.mate)
+
+    def hops(way, q):
+        return 4 if q % 2 == way else 3
+
+    for q in range(NB):
+        for d in range(len(place.peers)):
+            guarded(need(place.f, q), lambda: peer_copy(d, q).start())
+    for q in range(NB):
+        def own():
+            for d in range(len(place.peers)):
+                peer_copy(d, q).wait_recv()
+            for way in range(2):
+                ring_copy(way, 0, q)[1].start()
+            mate_copy(place.f, 0, q).start()
+        guarded(need(place.f, q), own)
+    for hop in range(1, 5):
+        for q in range(NB):
+            for way in range(2):
+                if hop > hops(way, q):
+                    continue
+                origin, copy = arrival(way, hop, q)
+                slot = hop if way == 0 else NB - hop
+                def take():
+                    copy.wait_recv()
+                    if hop < hops(way, q):
+                        ring_copy(way, hop, q)[1].start()
+                    mate_copy(origin, slot, q).start()
+                guarded(need(origin, q), take)
+    for slot in range(NB):
+        origin = lax.rem(place.f + NB - slot, NB)
+        for q in range(NB):
+            def close():
+                copy = mate_copy(origin, slot, q)
+                copy.wait_send()
+                copy.wait_recv()
+            guarded(need(origin, q), close)
+    for q in range(NB):
+        for way in range(2):
+            for hop in range(hops(way, q)):
+                origin, copy = ring_copy(way, hop, q)
+                guarded(need(origin, q), lambda: copy.wait_send())
+        for d in range(len(place.peers)):
+            guarded(need(place.f, q), lambda: peer_copy(d, q).wait_send())
+
+
+def assemble_kernel(height, update, entries, routes, whole, low, high, got, ex, *sems):
+    place = Place(height)
+    m = place.m
+    bit = lax.rem(place.leaf // 2 ** (height - 1), 2)
+    sibling = place.flip(2 ** (height - 1))
+    place.greet()
+    out_rows = pl.ds(pl.multiple_of((1 - bit) * m, m), m)
+    own_rows = pl.ds(pl.multiple_of(bit * m, m), m)
+    swap = remote(update.at[out_rows], got, ex.at[0], ex.at[1], sibling)
+    swap.start()
+    front = place.leaf // 2**height
+
+    def upper(child, j):
+        return jnp.where(routes[front, child, j] >= NB, 1.0, 0.0)
+
+    mine = pl.ds(pl.multiple_of(place.piece * m, m), m)
+    row_own = upper(bit, place.f)
+    row_other = upper(1 - bit, place.f)
+    for j in range(NB):
+        cols = pl.ds(j * BLK, BLK)
+        kept = update[own_rows, cols]
+        up = upper(bit, j)
+        whole[place.f, mine, cols] = entries[:m, cols] + ((1.0 - row_own) * (1.0 - up)) * kept
+        low[:, cols] = entries[m:, cols] + (row_own * (1.0 - up)) * kept
+        high[:, cols] = (row_own * up) * kept
+    swap.wait()
+    for j in range(NB):
+        cols = pl.ds(j * BLK, BLK)
+        other = got[:, cols]
+        up = upper(1 - bit, j)
+        whole[place.f, mine, cols] = whole[place.f, mine, cols] + ((1.0 - row_other) * (1.0 - up)) * other
+        low[:, cols] = low[:, cols] + (row_other * (1.0 - up)) * other
+        high[:, cols] = high[:, cols] + (row_other * up) * other
+    gather(place, whole, sems, True)
+
+
+def assemble_gather(height, update, entries, routes):
+    m = BLK >> height
+    vm = pl.BlockSpec(memory_space=pltpu.VMEM)
+    sm = pl.BlockSpec(memory_space=pltpu.SMEM)
+    f32 = jnp.float32
+    return pl.pallas_call(
+        functools.partial(assemble_kernel, height),
+        out_shape=(
+            jax.ShapeDtypeStruct((NB, BLK, 1024), f32),
+            jax.ShapeDtypeStruct((m, 1024), f32),
+            jax.ShapeDtypeStruct((m, 1024), f32),
+        ),
+        in_specs=[vm, vm, sm],
+        out_specs=(vm, vm, vm),
+        scratch_shapes=[pltpu.VMEM((m, 1024), f32), pltpu.SemaphoreType.DMA((2,))] + GATHER_SEMS,
+        compiler_params=pltpu.CompilerParams(collective_id=2 * height, has_side_effects=True, vmem_limit_bytes=40 * 2**20),
+        name="assemble_gather",
+    )(update, entries, routes)
+
+
+def schur_kernel(height, panel, high, out, whole, own, *sems):
+    place = Place(height)
+    m = place.m
+    place.greet()
+    mine = pl.ds(pl.multiple_of(place.piece * m, m), m)
+    for q in range(NB):
+        whole[place.f, mine, pl.ds(q * BLK, BLK)] = panel[:, q * BLK : (q + 1) * BLK]
+    gather(place, whole, sems, False)
+    ph, plo = split(panel[...])
+    for j in range(NB):
+        xh, xl = split(whole[j])
+        upd = dott(ph, xh) + (dott(ph, xl) + dott(plo, xh))
+        out[:, j * BLK : (j + 1) * BLK] = high[:, j * BLK : (j + 1) * BLK] - upd
+
+
+def schur_gather(height, panel, high):
+    m = BLK >> height
+    vm = pl.BlockSpec(memory_space=pltpu.VMEM)
+    f32 = jnp.float32
+    return pl.pallas_call(
+        functools.partial(schur_kernel, height),
+        out_shape=jax.ShapeDtypeStruct((m, 1024), f32),
+        in_specs=[vm, vm],
+        out_specs=vm,
+        scratch_shapes=[pltpu.VMEM((NB, BLK, 1024), f32), pltpu.VMEM((8, 128), f32)] + GATHER_SEMS,
+        compiler_params=pltpu.CompilerParams(collective_id=2 * height + 1, has_side_effects=True, vmem_limit_bytes=40 * 2**20),
+        name="schur_gather",
+    )(panel, high)
+
+
+def own_rows(height, lower_factor):
+    place = Place(height)
+    start = place.f * BLK + place.piece * place.m
+    return lax.dynamic_slice_in_dim(lower_factor, start, place.m, 0)
 
 
 def local(
@@ -173,63 +352,18 @@
     assembly_middle,
     assembly_upper,
 ):
-    front_count = lax.axis_size("front")
-    local_count = PIVOT_BLOCKS // front_count
-    leaf_index = lax.axis_index("leaf")
-    front_index = lax.axis_index("front")
-    pivot_size = leaf_contrib.shape[1]
-    update = leaf_contrib.reshape(local_count, BLK, pivot_size)
-    my_blocks = front_index + front_count * jnp.arange(local_count, dtype=jnp.int32)
-    selector = (jnp.arange(PIVOT_BLOCKS, dtype=jnp.int32)[None, :] == my_blocks[:, None]).astype(
-        jnp.float32
-    )
+    update = leaf_contrib
     results = []
     for height, entries, routes in (
         (1, entries_lower, assembly_lower),
         (2, entries_middle, assembly_middle),
         (3, entries_upper, assembly_upper),
     ):
-        piece_rows = BLK // 2**height
-        child_bit = leaf_index >> height - 1 & 1
-        low_rows = update[:, :piece_rows]
-        high_rows = update[:, piece_rows:]
-        kept = jnp.where(child_bit == 0, low_rows, high_rows)
-        outgoing = jnp.where(child_bit == 0, high_rows, low_rows)
-        received = partner_2(outgoing, "leaf", height - 1)
-        route_pair = lax.dynamic_index_in_dim(routes, leaf_index >> height, 0, keepdims=False)
-        upper_masks = (route_pair >= PIVOT_BLOCKS).astype(jnp.float32)
-        own_mask = jnp.where(child_bit == 0, upper_masks[0], upper_masks[1])
-        other_mask = jnp.where(child_bit == 0, upper_masks[1], upper_masks[0])
-        slab_rows = local_count * piece_rows
-        pivot_slab = entries[:slab_rows].reshape(local_count, piece_rows, pivot_size)
-        update_slab = jnp.zeros((local_count, piece_rows, 2 * pivot_size), jnp.float32)
-        update_slab = update_slab.at[:, :, :pivot_size].set(
-            entries[slab_rows:].reshape(local_count, piece_rows, pivot_size)
-        )
-        for contribution, column_mask in ((kept, own_mask), (received, other_mask)):
-            spread = spread_columns(contribution, column_mask)
-            row_upper = jnp.sum(selector * column_mask[None, :], axis=1)
-            pivot_slab = pivot_slab + (1.0 - row_upper)[:, None, None] * spread[:, :, :pivot_size]
-            update_slab = update_slab + row_upper[:, None, None] * spread
-        piece_index = reversed_bits(leaf_index & 2**height - 1, height)
-        update_pivot = update_slab[:, :, :pivot_size]
-        whole_pivot = group_gather(pivot_slab, height).reshape(pivot_size, pivot_size)
-        lower_factor, own_panel = factor_panel(whole_pivot, update_pivot.reshape(-1, pivot_size))
-        all_panel = group_gather(
-            own_panel.reshape(local_count, piece_rows, pivot_size), height
-        ).reshape(pivot_size, pivot_size)
-        own_factor = own_rows(
-            lower_factor.reshape(local_count, front_count, BLK, pivot_size),
-            front_index,
-            piece_index,
-            piece_rows,
-        ).reshape(-1, pivot_size)
-        results.append(jnp.concatenate([own_factor, own_panel], axis=0))
-        schur_rows = update_slab[:, :, pivot_size:].reshape(-1, pivot_size) - product(
-            own_panel, all_panel.T
-        )
-        update = schur_rows.reshape(local_count, piece_rows, pivot_size)
-    return (results[0], results[1], results[2], update.reshape(-1, pivot_size))
+        whole, low, high = assemble_gather(height, update, entries, routes)
+        lower_factor, panel = factor_panel(whole.reshape(1024, 1024), low)
+        update = schur_gather(height, panel, high)
+        results.append(jnp.concatenate([own_rows(height, lower_factor), panel], axis=0))
+    return (results[0], results[1], results[2], update)
 
 
 def solution(mesh):

time: 541 us -> 343 us (0.63)
  waiting for transfers between devices: 242 us -> 0 us
  Pallas kernels: 119 us -> 316 us
  starting transfers between devices: 58.8 us -> 0 us
  blocking collectives: 39.2 us -> 0 us
  other arithmetic: 36.9 us -> 2.23 us
  between operations: 18.6 us -> 1.24 us
  matrix products: 12.3 us -> 0 us
  local copies, waits for them, and re-layouts: 5.53 us -> 16.8 us
    pallas_call x0 -> x6, Pallas kernels: none -> 197 us  [the longest x3 98.9 us: schur_gather(): pl.pallas_call(functools.partial(schur_kernel, height), out_shape=jax.Sha...]
    all_gather x4 -> x0, waiting for transfers between devices: 139 us -> none  [group_gather(): gathered = lax.all_gather(pieces[:, None], 'front', axis=1, tiled=True)]
    ppermute x15 -> x0, waiting for transfers between devices: 103 us -> none  [partner_2(): return lax.ppermute(value, axis, pairs)]
    ppermute x15 -> x0, starting transfers between devices: 58.7 us -> none  [partner_2(): return lax.ppermute(value, axis, pairs)]
    all_gather x2 -> x0, blocking collectives: 39.2 us -> none  [group_gather(): gathered = lax.all_gather(pieces[:, None], 'front', axis=1, tiled=True)]
    select_n x12 -> x0, other arithmetic: 23.7 us -> none  [join_pieces(): jnp.where(upper_bit == 0, jnp.concatenate([mine, theirs], axis_index), jn...]
    unnamed x23 -> x32, local copies, waits for them, and re-layouts: 0.32 us -> 14 us
    dot_general x3 -> x0, matrix products: 12.3 us -> none  [product(): jnp.dot(left, right, precision=lax.Precision.HIGHEST, preferred_element_t...]
  transfers between devices with their start and end apart: 19 -> 0, of which waited for: 17 -> 0; matrix products, arithmetic and copies ran while one was open for 3% -> 0% of each run, Pallas kernels for 0% -> 0%
where the time goes in v2:
time: 343 us; the launch traced here: 337 us
  Pallas kernels  316 us (92%)
  local copies, waits for them, and re-layouts  16.8 us (5%)
    pallas_call x3, Pallas kernels, factor_panel(): pl.pallas_call(functools.partial(kernel, m), out_shape=(jax.ShapeDtypeStr...  119 us
    pallas_call x3, Pallas kernels, schur_gather(): pl.pallas_call(functools.partial(schur_kernel, height), out_shape=jax.Sha...  98.9 us
    pallas_call x3, Pallas kernels, assemble_gather(): pl.pallas_call(functools.partial(assemble_kernel, height), out_shape=(jax...  98.4 us
    unnamed x32, local copies, waits for them, and re-layouts  14 us

profile of v2, /device:TPU:1, one launch (start us, length us, event | category | flops | bytes accessed | tf_op | source)
XLA Modules:
  0.0 336.6 jit_solution(12133358430529530590)
XLA Ops:
  0.6 0.0 copy-start.13
  0.8 0.8 copy.11.routes
  1.5 0.0 copy-start.4
  1.5 1.0 copy-done.4
  2.6 0.0 copy-start.5
  2.6 1.0 copy-done.5
  3.6 0.0 copy-start.8
  3.6 32.1 %assemble_gather.3 = (f32[8,128,1024]{2,1,0:T(8,128)S(1)}, f32[64,1024]{1,0:T(8,128)S(1)}, f32[64,1024]{1,0:T(8,128)S(1)}) custom-call(f32[128,1024]{1,0:T(8,128)S(1)} %copy-done.4, f32[128,1024]{1,0:T(8,128)S(1)} %copy-done.5, s32[16,2,8]{2,1,0:T(2,128)S(1)} %copy.11.routes), custom_call_target="tpu_custom_call" | custom-call | tf_op jit(solution)/shard_map/assemble_gather/pallas_call | solution.py:295
  35.8 0.0 copy-start
  35.8 1.9 copy-done
  37.7 0.0 copy-start.7
  37.7 0.7 copy-done.7
  38.4 39.6 %factor_panel.3 = (f32[1024,1024]{1,0:T(8,128)}, f32[64,1024]{1,0:T(8,128)}) custom-call(f32[1024,1024]{1,0:T(8,128)} %bitcast.3, f32[64,1024]{1,0:T(8,128)} %copy-done.7), custom_call_target="tpu_custom_call" | custom-call | tf_op jit(solution)/shard_map/factor_panel/pallas_call | solution.py:105
  78.1 0.0 copy-start.11
  78.1 0.0 copy-start.14
  78.1 1.0 constant_dynamic-slice_fusion.2
  79.1 0.0 copy-start.3
  79.1 0.9 copy-done.3
  80.0 30.2 %schur_gather.3.update = f32[64,1024]{1,0:T(8,128)S(1)} custom-call(f32[64,1024]{1,0:T(8,128)S(1)} %copy-done.3, f32[64,1024]{1,0:T(8,128)S(1)} %get-tuple-element.23.high), custom_call_target="tpu_custom_call" | custom-call | tf_op jit(solution)/shard_map/schur_gather/pallas_call | solution.py:329
  110.3 0.8 pad_maximum_fusion
  111.1 0.0 copy-done.13
  111.1 0.0 copy-done.8
  111.1 32.5 %assemble_gather.4 = (f32[8,128,1024]{2,1,0:T(8,128)S(1)}, f32[32,1024]{1,0:T(8,128)S(1)}, f32[32,1024]{1,0:T(8,128)S(1)}) custom-call(f32[64,1024]{1,0:T(8,128)S(1)} %schur_gather.3.update, f32[64,1024]{1,0:T(8,128)S(1)} %copy-done.8, s32[8,2,8]{2,1,0:T(2,128)S(1)} %copy-done.13), custom_call_target="tpu_custom_call" | custom-call | tf_op jit(solution)/shard_map/assemble_gather/pallas_call | solution.py:295
  143.7 0.0 copy-start.1
  143.7 1.9 copy-done.1
  145.6 0.0 copy-start.10
  145.6 0.7 copy-done.10
  146.3 39.4 %factor_panel.4 = (f32[1024,1024]{1,0:T(8,128)}, f32[32,1024]{1,0:T(8,128)}) custom-call(f32[1024,1024]{1,0:T(8,128)} %bitcast.4, f32[32,1024]{1,0:T(8,128)} %copy-done.10), custom_call_target="tpu_custom_call" | custom-call | tf_op jit(solution)/shard_map/factor_panel/pallas_call | solution.py:105
  185.6 0.9 constant_dynamic-slice_fusion.1
  186.5 0.0 copy-start.6
  186.5 0.9 copy-done.6
  187.4 33.9 %schur_gather.4.update = f32[32,1024]{1,0:T(8,128)S(1)} custom-call(f32[32,1024]{1,0:T(8,128)S(1)} %copy-done.6, f32[32,1024]{1,0:T(8,128)S(1)} %get-tuple-element.28.high), custom_call_target="tpu_custom_call" | custom-call | tf_op jit(solution)/shard_map/schur_gather/pallas_call | solution.py:329
  221.4 0.7 pad_maximum_fusion.1
  222.1 0.0 copy-done.11
  222.1 0.0 copy-done.14
  222.1 33.7 %assemble_gather.5 = (f32[8,128,1024]{2,1,0:T(8,128)S(1)}, f32[16,1024]{1,0:T(8,128)S(1)}, f32[16,1024]{1,0:T(8,128)S(1)}) custom-call(f32[32,1024]{1,0:T(8,128)S(1)} %schur_gather.4.update, f32[32,1024]{1,0:T(8,128)S(1)} %copy-done.11, s32[4,2,8]{2,1,0:T(2,128)S(1)} %copy-done.14), custom_call_target="tpu_custom_call" | custom-call | tf_op jit(solution)/shard_map/assemble_gather/pallas_call | solution.py:295
  255.8 0.0 copy-start.2
  255.8 1.9 copy-done.2
  257.8 0.0 copy-start.12
  257.8 0.6 copy-done.12
  258.4 40.1 %factor_panel.5 = (f32[1024,1024]{1,0:T(8,128)}, f32[16,1024]{1,0:T(8,128)}) custom-call(f32[1024,1024]{1,0:T(8,128)} %bitcast.5, f32[16,1024]{1,0:T(8,128)} %copy-done.12), custom_call_target="tpu_custom_call" | custom-call | tf_op jit(solution)/shard_map/factor_panel/pallas_call | solution.py:105
  298.5 0.8 constant_dynamic-slice_fusion
  299.4 0.0 copy-start.9
  299.4 0.8 copy-done.9
  300.2 34.7 %schur_gather.5 = f32[16,1024]{1,0:T(8,128)S(1)} custom-call(f32[16,1024]{1,0:T(8,128)S(1)} %copy-done.9, f32[16,1024]{1,0:T(8,128)S(1)} %get-tuple-element.33.high), custom_call_target="tpu_custom_call" | custom-call | tf_op jit(solution)/shard_map/schur_gather/pallas_call | solution.py:329
  334.9 0.7 pad_maximum_fusion.2
  335.6 0.6 copy.13
Async XLA Ops:
  0.6 110.5 %copy-start.13 = (s32[8,2,8]{2,1,0:T(2,128)S(1)}, s32[8,2,8]{2,1,0:T(2,128)}, u32[]{:S(2)}) copy-start(s32[8,2,8]{2,1,0:T(2,128)} %routes.3) | copy-start | bytes 1540
  1.5 1.0 copy-start.4
  2.6 1.0 copy-start.5
  3.6 107.5 %copy-start.8 = (f32[64,1024]{1,0:T(8,128)S(1)}, f32[64,1024]{1,0:T(8,128)}, u32[]{:S(2)}) copy-start(f32[64,1024]{1,0:T(8,128)} %entries.4) | copy-start | bytes 786436
  35.8 1.9 copy-start
  37.7 0.7 copy-start.7
  78.1 144.0 %copy-start.11 = (f32[32,1024]{1,0:T(8,128)S(1)}, f32[32,1024]{1,0:T(8,128)}, u32[]{:S(2)}) copy-start(f32[32,1024]{1,0:T(8,128)} %entries.5) | copy-start | bytes 393220
  78.1 144.0 %copy-start.14 = (s32[4,2,8]{2,1,0:T(2,128)S(1)}, s32[4,2,8]{2,1,0:T(2,128)}, u32[]{:S(2)}) copy-start(s32[4,2,8]{2,1,0:T(2,128)} %routes.4) | copy-start | bytes 772
  79.1 1.0 copy-start.3
  143.7 1.9 copy-start.1
  145.6 0.7 copy-start.10
  186.5 0.9 copy-start.6
  255.8 1.9 copy-start.2
  257.8 0.6 copy-start.12
  299.4 0.8 copy-start.9

commit v3 on v2

v3 whole, which is shorter than its diff:
```python
import functools

import jax
import jax.numpy as jnp
from jax import lax
from jax.experimental import pallas as pl
from jax.experimental.pallas import tpu as pltpu
from jax.sharding import PartitionSpec as P

BLK = 128
SB = 16

def split(x):
    h = x.astype(jnp.bfloat16)
    return h, (x - h.astype(jnp.float32)).astype(jnp.bfloat16)

def dotb(a, b):
    return jnp.dot(a, b, preferred_element_type=jnp.float32)

def dott(a, b):
    return lax.dot_general(a, b, (((1,), (1,)), ((), ())), preferred_element_type=jnp.float32)

def substep(g_ref, u_ref, s):
    base = s * SB
    p = g_ref[base:base + SB, :]
    cols = [jnp.broadcast_to(p[:, base + k:base + k + 1], (SB, 128)) for k in range(SB)]
    pl_, pr_ = p[:, :128], p[:, 128:]
    sub = lax.broadcasted_iota(jnp.int32, (SB, 128), 0)
    ul = jnp.zeros((SB, 128), jnp.float32)
    ur = jnp.zeros((SB, 128), jnp.float32)
    for r in range(SB):
        hit = sub == r
        v = cols[r]
        piv = jnp.broadcast_to(v[r:r + 1], (SB, 128))
        rs = lax.rsqrt(piv)
        inv = rs * rs
        rl = jnp.broadcast_to(pl_[r:r + 1], (SB, 128))
        rr = jnp.broadcast_to(pr_[r:r + 1], (SB, 128))
        ul = jnp.where(hit, rl * rs, ul)
        ur = jnp.where(hit, rr * rs, ur)
        vi = jnp.where(hit, 0.0, v * inv)
        for k in range(r + 1, SB):
            c = jnp.broadcast_to(cols[k][r:r + 1], (SB, 128))
            cols[k] = jnp.where(hit, c * inv, cols[k] - vi * c)
        pl_ = jnp.where(hit, rl * inv, pl_ - vi * rl)
        pr_ = jnp.where(hit, rr * inv, pr_ - vi * rr)
    u_ref[base:base + SB, :128] = ul
    u_ref[base:base + SB, 128:] = ur
    if s < 128 // SB - 1:
        lo = base + SB
        R = jnp.concatenate([pl_, pr_], 1)
        rh, rlo = split(R)
        parts = []
        def pad(x):
            z = []
            if base: z.append(jnp.zeros((base, 256), jnp.bfloat16))
            z.append(x)
            if 128 - lo: z.append(jnp.zeros((128 - lo, 256), jnp.bfloat16))
            return jnp.concatenate(z, 0)
        d = g_ref[lo:, :128]
        dh, dl = split(d)
        upd = dotb(jnp.concatenate([dh, dl], 1), jnp.concatenate([pad(rh), pad(rh)], 0)) + dotb(dh, pad(rlo))
        g_ref[lo:, :] = g_ref[lo:, :] - upd


MESH = pl.DeviceIdType.MESH
NB = 8


class Place:
    def __init__(self, height):
        self.m = BLK >> height
        self.leaf = lax.axis_index("leaf")
        self.f = lax.axis_index("front")
        self.core = lax.rem(self.leaf, 2)
        member = lax.rem(self.leaf, 2**height)
        piece = 0
        for bit in range(height):
            piece = piece + lax.rem(member // 2**bit, 2) * 2 ** (height - 1 - bit)
        self.piece = piece
        self.peers = [self.flip(2 * d) for d in range(1, 2 ** (height - 1))]
        self.mate = self.flip(1)
        self.right = (self.leaf, lax.rem(self.f + 1, NB))
        self.left = (self.leaf, lax.rem(self.f + NB - 1, NB))

    def flip(self, mask):
        other = self.leaf
        bit = 1
        while bit <= mask:
            if mask & bit:
                other = other + bit * (1 - 2 * lax.rem(self.leaf // bit, 2))
            bit *= 2
        return (other, self.f)

    def greet(self):
        barrier = pltpu.get_barrier_semaphore()
        others = [self.left, self.right, self.mate] + self.peers
        for other in others:
            pl.semaphore_signal(barrier, inc=1, device_id=other, device_id_type=MESH)
        pl.semaphore_wait(barrier, len(others))

    def before(self, hop, way):
        return lax.rem(self.f + ((NB - hop) if way == 0 else hop), NB)


def guarded(conds, body):
    live = [c for c in conds if c is not True]
    if any(c is False for c in live):
        return
    if not live:
        body()
        return
    both = live[0]
    for c in live[1:]:
        both = jnp.logical_and(both, c)
    pl.when(both)(body)


def remote(src, dst, send, recv, device):
    return pltpu.make_async_remote_copy(
        src_ref=src, dst_ref=dst, send_sem=send, recv_sem=recv, device_id=device, device_id_type=MESH
    )


GATHER_SEMS = [
    pltpu.SemaphoreType.DMA((3, NB)),
    pltpu.SemaphoreType.DMA((3, NB)),
    pltpu.SemaphoreType.DMA((2, 4, NB)),
    pltpu.SemaphoreType.DMA((2, 4, NB)),
    pltpu.SemaphoreType.DMA((NB, NB)),
    pltpu.SemaphoreType.DMA((NB, NB)),
]


class Gather:
    def __init__(self, place, buf, sems, lower):
        self.place, self.buf, self.sems, self.lower = place, buf, sems, lower

    def need(self, origin, q):
        if not self.lower or (isinstance(q, int) and q == 0):
            return True
        return origin >= q

    def slab(self, origin, q):
        start = pl.multiple_of(origin * BLK + self.place.core * 64, 64)
        return self.buf.at[q, pl.ds(start, 64), :]

    def peer_copy(self, d, q):
        p = self.place
        mine = self.buf.at[q, pl.ds(pl.multiple_of(p.f * BLK + p.piece * p.m, p.m), p.m), :]
        return remote(mine, mine, self.sems[0].at[d, q], self.sems[1].at[d, q], p.peers[d])

    def ring_copy(self, way, hop, q, origin):
        p = self.place
        mine = self.slab(origin, q)
        return remote(mine, mine, self.sems[2].at[way, hop, q], self.sems[3].at[way, hop, q], (p.right, p.left)[way])

    def mate_copy(self, origin, slot, q):
        mine = self.slab(origin, q)
        return remote(mine, mine, self.sems[4].at[slot, q], self.sems[5].at[slot, q], self.place.mate)

    def post(self, q, *conds):
        def body():
            for d in range(len(self.place.peers)):
                self.peer_copy(d, q).start()
        if self.place.peers:
            guarded([self.need(self.place.f, q), *conds], body)

    def begin(self, q, *conds):
        def body():
            for d in range(len(self.place.peers)):
                self.peer_copy(d, q).wait_recv()
            for way in range(2):
                self.ring_copy(way, 0, q, self.place.f).start()
            self.mate_copy(self.place.f, 0, q).start()
        guarded([self.need(self.place.f, q), *conds], body)

    def last(self, way, q):
        return q % 2 == way if isinstance(q, int) else lax.rem(q, 2) == way

    def hop(self, h, q, *conds):
        for way in range(2):
            origin = self.place.before(h, way)
            slot = h if way == 0 else NB - h
            def body():
                self.ring_copy(way, h - 1, q, origin).wait_recv()
                if h < 3:
                    self.ring_copy(way, h, q, origin).start()
                elif h == 3:
                    guarded([self.last(way, q)], lambda: self.ring_copy(way, 3, q, origin).start())
                self.mate_copy(origin, slot, q).start()
            guarded([self.need(origin, q), self.last(way, q) if h == 4 else True, *conds], body)

    def land(self, q):
        for slot in range(NB):
            origin = self.place.before(slot, 0)
            guarded([self.need(origin, q)], lambda: self.mate_copy(origin, slot, q).wait_recv())

    def close(self):
        def each(q, _):
            for slot in range(NB):
                origin = self.place.before(slot, 0)
                guarded([self.need(origin, q)], lambda: self.mate_copy(origin, slot, q).wait_send())
            for way in range(2):
                for h in range(4):
                    origin = self.place.before(h, way)
                    guarded(
                        [self.need(origin, q), self.last(way, q) if h == 3 else True],
                        lambda: self.ring_copy(way, h, q, origin).wait_send(),
                    )
            def peers():
                for d in range(len(self.place.peers)):
                    self.peer_copy(d, q).wait_send()
            if self.place.peers:
                guarded([self.need(self.place.f, q)], peers)
            return 0
        lax.fori_loop(0, NB, each, 0)


def level_kernel(height, update, entries, routes, fac, out, whole, pan, low, got, xh, xl, col, g_ref, u_ref, ex, *sems):
    place = Place(height)
    m = place.m
    f = place.f
    bit = lax.rem(place.leaf // 2 ** (height - 1), 2)
    sibling = place.flip(2 ** (height - 1))
    place.greet()
    out_rows = pl.ds(pl.multiple_of((1 - bit) * m, m), m)
    own_rows = pl.ds(pl.multiple_of(bit * m, m), m)
    swap = remote(update.at[out_rows], got, ex.at[0], ex.at[1], sibling)
    swap.start()
    front = place.leaf // 2**height

    def upper(child, j):
        return jnp.where(routes[front, child, j] >= NB, 1.0, 0.0)

    mine = pl.ds(pl.multiple_of(f * BLK + place.piece * m, m), m)
    row_own = upper(bit, f)
    row_other = upper(1 - bit, f)
    for j in range(NB):
        cols = pl.ds(j * BLK, BLK)
        kept = update[own_rows, cols]
        up = upper(bit, j)
        col[j * m : (j + 1) * m, :] = entries[:m, cols] + ((1.0 - row_own) * (1.0 - up)) * kept
        low[:, cols] = entries[m:, cols] + (row_own * (1.0 - up)) * kept
        out[:, cols] = (row_own * up) * kept
    fac[:m, :] = jnp.zeros((m, 1024), jnp.float32)
    swap.wait()
    for j in range(NB):
        other = got[:, j * BLK : (j + 1) * BLK]
        up = upper(1 - bit, j)
        whole[j, mine, :] = col[j * m : (j + 1) * m, :] + ((1.0 - row_other) * (1.0 - up)) * other
    pivots = Gather(place, whole, sems[:6], True)
    panels = Gather(place, pan, sems[6:], False)
    for q in range(NB):
        pivots.post(q)
    for j in range(NB):
        cols = pl.ds(j * BLK, BLK)
        other = got[:, cols]
        up = upper(1 - bit, j)
        low[:, cols] = low[:, cols] + (row_other * (1.0 - up)) * other
        out[:, cols] = out[:, cols] + (row_other * up) * other

    def wave(w):
        for h in range(4, -1, -1):
            q = w - h
            if 0 <= q < NB:
                if h:
                    pivots.hop(h, q)
                else:
                    pivots.begin(q)

    for w in range(5):
        wave(w)

    lane = lax.broadcasted_iota(jnp.int32, (BLK, BLK), 1)
    row = lax.broadcasted_iota(jnp.int32, (BLK, BLK), 0)

    def accumulate(q):
        panels.land(q)
        ph, plo = split(fac[m:, pl.ds(pl.multiple_of(q * BLK, BLK), BLK)])
        th, tl = split(pan[q])
        out[...] = out[...] - (dott(ph, th) + (dott(ph, tl) + dott(plo, th)))

    waves = {1: 5, 4: 6, 7: 7, 10: 8, 13: 9, 16: 10, 19: 11}
    first = 1 if height == 1 else 2

    def slot(k, s):
        for t, w in waves.items():
            if t % 8 == s:
                pl.when(k == t // 8)(lambda: wave(w))
        if s == 0:
            panels.post(k - 1, k >= 1)
            panels.hop(2, k - 2, k >= 2)
        if s == first:
            panels.begin(k - 1, k >= 1)
        if s == 5:
            panels.hop(1, k - 1, k >= 1)
        if s == 3:
            panels.hop(3, k - 2, k >= 2)
        if s == 6:
            panels.hop(4, k - 2, k >= 2)
        if s == 7:
            pl.when(k >= 3)(lambda: accumulate(k - 3))

    def step(k, _):
        pivots.land(k)
        for kk in range(NB):
            @pl.when(k == kk)
            def _():
                c = jnp.concatenate([whole[kk, kk * BLK :, :], low[:, kk * BLK : (kk + 1) * BLK]], 0)
                if kk:
                    K = kk * BLK
                    rh, rl = xh[K : K + BLK, :K], xl[K : K + BLK, :K]
                    c = c - (dott(xh[K:, :K], rh) + (dott(xh[K:, :K], rl) + dott(xl[K:, :K], rh)))
                g_ref[:, :BLK] = c[:BLK]
                col[kk * BLK + BLK :, :] = c[BLK:]
        g_ref[:, BLK:] = jnp.where(lane == row, 1.0, 0.0)
        for s in range(BLK // SB):
            substep(g_ref, u_ref, s)
            slot(k, s)
        col[pl.ds(pl.multiple_of(k * BLK, BLK), BLK), :] = jnp.where(lane <= row, u_ref[:, :BLK].T, 0.0)
        wh, wl = split(u_ref[:, BLK:])
        for kk in range(NB):
            @pl.when(k == kk)
            def _():
                K = kk * BLK
                ch, cl = split(col[K + BLK :, :])
                x = dott(ch, wh) + (dott(ch, wl) + dott(cl, wh))
                if kk < NB - 1:
                    col[K + BLK : 1024, :] = x[: 1024 - K - BLK]
                tail = x[1024 - K - BLK :]
                fac[m:, K : K + BLK] = tail
                pan[kk, mine, :] = tail
                h, l = split(x)
                xh[K + BLK :, K : K + BLK] = h
                xl[K + BLK :, K : K + BLK] = l

        @pl.when(f >= k)
        def _():
            fac[:m, pl.ds(pl.multiple_of(k * BLK, BLK), BLK)] = col[mine, :]

        return 0

    lax.fori_loop(0, NB, step, 0)
    panels.post(7)
    panels.hop(2, 6)
    accumulate(5)
    panels.begin(7)
    panels.hop(3, 6)
    panels.hop(1, 7)
    panels.hop(4, 6)
    panels.hop(2, 7)
    panels.hop(3, 7)
    accumulate(6)
    panels.hop(4, 7)
    accumulate(7)
    pivots.close()
    panels.close()


def level(height, update, entries, routes):
    m = BLK >> height
    vm = pl.BlockSpec(memory_space=pltpu.VMEM)
    sm = pl.BlockSpec(memory_space=pltpu.SMEM)
    f32, bf16 = jnp.float32, jnp.bfloat16
    return pl.pallas_call(
        functools.partial(level_kernel, height),
        out_shape=(jax.ShapeDtypeStruct((2 * m, 1024), f32), jax.ShapeDtypeStruct((m, 1024), f32)),
        in_specs=[vm, vm, sm],
        out_specs=(vm, vm),
        scratch_shapes=[
            pltpu.VMEM((NB, 1024, BLK), f32),
            pltpu.VMEM((NB, 1024, BLK), f32),
            pltpu.VMEM((m, 1024), f32),
            pltpu.VMEM((m, 1024), f32),
            pltpu.VMEM((1024 + m, 1024), bf16),
            pltpu.VMEM((1024 + m, 1024), bf16),
            pltpu.VMEM((1024 + m, BLK), f32),
            pltpu.VMEM((BLK, 2 * BLK), f32),
            pltpu.VMEM((BLK, 2 * BLK), f32),
            pltpu.SemaphoreType.DMA((2,)),
        ]
        + GATHER_SEMS
        + GATHER_SEMS,
        compiler_params=pltpu.CompilerParams(
            collective_id=height, has_side_effects=True, vmem_limit_bytes=48 * 2**20
        ),
        name="front_level",
    )(update, entries, routes)


def local(
    leaf_contrib,
    entries_lower,
    entries_middle,
    entries_upper,
    assembly_lower,
    assembly_middle,
    assembly_upper,
):
    lower, update = level(1, leaf_contrib, entries_lower, assembly_lower)
    middle, update = level(2, update, entries_middle, assembly_middle)
    upper, update = level(3, update, entries_upper, assembly_upper)
    return (lower, middle, upper, update)


def solution(mesh):
    in_specs = (
        P(("leaf", "front"), None),
        P(("leaf", "front"), None),
        P(("leaf", "front"), None),
        P(("leaf", "front"), None),
        P(),
        P(),
        P(),
    )
    out_specs = (
        P(("leaf", "front"), None),
        P(("leaf", "front"), None),
        P(("leaf", "front"), None),
        P(("leaf", "front"), None),
    )
    return jax.shard_map(local, mesh=mesh, in_specs=in_specs, out_specs=out_specs, check_vma=False)
```

time: 343 us -> 376 us (1.096); the launches traced: 337 us -> 376 us
  Pallas kernels: 316 us -> 370 us
  local copies, waits for them, and re-layouts: 16.8 us -> 5.66 us
    pallas_call x9 -> x3, Pallas kernels: 316 us -> 370 us  [level(): pl.pallas_call(functools.partial(level_kernel, height), out_shape=(jax.Sh...]
    unnamed x32 -> x17, local copies, waits for them, and re-layouts: 14 us -> 5.66 us
where the time goes in v3:
time: 376 us
  Pallas kernels  370 us (98%)
  local copies, waits for them, and re-layouts  5.66 us (2%)
    pallas_call x3, Pallas kernels, level(): pl.pallas_call(functools.partial(level_kernel, height), out_shape=(jax.Sh...  370 us

profile of v3, /device:TPU:1, one launch (start us, length us, event | category | flops | bytes accessed | tf_op | source)
XLA Modules:
  0.0 375.9 jit_solution(2636723047838578378)
XLA Ops:
  0.6 0.8 copy.11.routes
  1.4 0.0 copy-start
  1.4 1.0 copy-done
  2.5 0.0 copy-start.1
  2.5 1.0 copy-done.1
  3.5 0.0 copy-start.2
  3.5 0.0 copy-start.4
  3.5 117.8 %front_level.3 = (f32[128,1024]{1,0:T(8,128)S(1)}, f32[64,1024]{1,0:T(8,128)S(1)}) custom-call(f32[128,1024]{1,0:T(8,128)S(1)} %copy-done, f32[128,1024]{1,0:T(8,128)S(1)} %copy-done.1, s32[16,2,8]{2,1,0:T(2,128)S(1)} %copy.11.routes), custom_call_target="tpu_custom_call" | custom-call | tf_op jit(solution)/shard_map/front_level/pallas_call | solution.py:366
  121.3 0.0 copy-done.2
  121.3 0.0 copy-done.4
  121.3 0.0 copy-start.3
  121.4 0.0 copy-start.5
  121.4 122.6 %front_level.4 = (f32[64,1024]{1,0:T(8,128)S(1)}, f32[32,1024]{1,0:T(8,128)S(1)}) custom-call(f32[64,1024]{1,0:T(8,128)S(1)} %get-tuple-element.11.update, f32[64,1024]{1,0:T(8,128)S(1)} %copy-done.2, s32[8,2,8]{2,1,0:T(2,128)S(1)} %copy-done.4), custom_call_target="tpu_custom_call" | custom-call | tf_op jit(solution)/shard_map/front_level/pallas_call | solution.py:366
  244.0 0.0 copy-done.3
  244.0 0.0 copy-done.5
  244.0 129.1 %front_level.5 = (f32[32,1024]{1,0:T(8,128)S(1)}, f32[16,1024]{1,0:T(8,128)S(1)}) custom-call(f32[32,1024]{1,0:T(8,128)S(1)} %get-tuple-element.13.update, f32[32,1024]{1,0:T(8,128)S(1)} %copy-done.3, s32[4,2,8]{2,1,0:T(2,128)S(1)} %copy-done.5), custom_call_target="tpu_custom_call" | custom-call | tf_op jit(solution)/shard_map/front_level/pallas_call | solution.py:366
  373.1 0.8 copy.16
  373.9 0.7 copy.17
  374.6 0.7 copy.18
  375.3 0.6 copy.19
Async XLA Ops:
  1.4 1.0 copy-start
  2.5 1.0 copy-start.1
  3.5 117.8 %copy-start.2 = (f32[64,1024]{1,0:T(8,128)S(1)}, f32[64,1024]{1,0:T(8,128)}, u32[]{:S(2)}) copy-start(f32[64,1024]{1,0:T(8,128)} %entries.4) | copy-start | bytes 786436
  3.5 117.8 %copy-start.4 = (s32[8,2,8]{2,1,0:T(2,128)S(1)}, s32[8,2,8]{2,1,0:T(2,128)}, u32[]{:S(2)}) copy-start(s32[8,2,8]{2,1,0:T(2,128)} %routes.3) | copy-start | bytes 1540
  121.3 122.6 %copy-start.3 = (f32[32,1024]{1,0:T(8,128)S(1)}, f32[32,1024]{1,0:T(8,128)}, u32[]{:S(2)}) copy-start(f32[32,1024]{1,0:T(8,128)} %entries.5) | copy-start | bytes 393220
  121.4 122.6 %copy-start.5 = (s32[4,2,8]{2,1,0:T(2,128)S(1)}, s32[4,2,8]{2,1,0:T(2,128)}, u32[]{:S(2)}) copy-start(s32[4,2,8]{2,1,0:T(2,128)} %routes.4) | copy-start | bytes 772

commit v4 on v3

v4 whole, which is shorter than its diff:
```python
import functools

import jax
import jax.numpy as jnp
from jax import lax
from jax.experimental import pallas as pl
from jax.experimental.pallas import tpu as pltpu
from jax.sharding import PartitionSpec as P

BLK = 128
SB = 16

def split(x):
    h = x.astype(jnp.bfloat16)
    return h, (x - h.astype(jnp.float32)).astype(jnp.bfloat16)

def dotb(a, b):
    return jnp.dot(a, b, preferred_element_type=jnp.float32)

def dott(a, b):
    return lax.dot_general(a, b, (((1,), (1,)), ((), ())), preferred_element_type=jnp.float32)

def substep(g_ref, u_ref, s):
    base = s * SB
    p = g_ref[base:base + SB, :]
    cols = [jnp.broadcast_to(p[:, base + k:base + k + 1], (SB, 128)) for k in range(SB)]
    pl_, pr_ = p[:, :128], p[:, 128:]
    sub = lax.broadcasted_iota(jnp.int32, (SB, 128), 0)
    ul = jnp.zeros((SB, 128), jnp.float32)
    ur = jnp.zeros((SB, 128), jnp.float32)
    for r in range(SB):
        hit = sub == r
        v = cols[r]
        piv = jnp.broadcast_to(v[r:r + 1], (SB, 128))
        rs = lax.rsqrt(piv)
        inv = rs * rs
        rl = jnp.broadcast_to(pl_[r:r + 1], (SB, 128))
        rr = jnp.broadcast_to(pr_[r:r + 1], (SB, 128))
        ul = jnp.where(hit, rl * rs, ul)
        ur = jnp.where(hit, rr * rs, ur)
        vi = jnp.where(hit, 0.0, v * inv)
        for k in range(r + 1, SB):
            c = jnp.broadcast_to(cols[k][r:r + 1], (SB, 128))
            cols[k] = jnp.where(hit, c * inv, cols[k] - vi * c)
        pl_ = jnp.where(hit, rl * inv, pl_ - vi * rl)
        pr_ = jnp.where(hit, rr * inv, pr_ - vi * rr)
    u_ref[base:base + SB, :128] = ul
    u_ref[base:base + SB, 128:] = ur
    lo = base + SB
    if lo < 128:
        near = g_ref[lo:lo + SB, :]
        sums = [near[:, :128], near[:, 128:]]
        parts = [None, None]
        for k in range(SB):
            dk = jnp.broadcast_to(near[:, base + k:base + k + 1], (SB, 128))
            tl = dk * jnp.broadcast_to(pl_[k:k + 1], (SB, 128))
            tr = dk * jnp.broadcast_to(pr_[k:k + 1], (SB, 128))
            if k % 2:
                sums = [sums[0] - tl, sums[1] - tr]
            else:
                parts = [tl, tr] if parts[0] is None else [parts[0] + tl, parts[1] + tr]
        g_ref[lo:lo + SB, :128] = sums[0] - parts[0]
        g_ref[lo:lo + SB, 128:] = sums[1] - parts[1]
    hi = lo + SB
    if hi < 128:
        rh, rlo = split(jnp.concatenate([pl_, pr_], 1))
        def pad(x):
            z = [jnp.zeros((base, 256), jnp.bfloat16)] if base else []
            return jnp.concatenate(z + [x, jnp.zeros((128 - lo, 256), jnp.bfloat16)], 0)
        dh, dl = split(g_ref[hi:, :128])
        ph = pad(rh)
        upd = dotb(jnp.concatenate([dh, dl], 1), jnp.concatenate([ph, ph], 0)) + dotb(dh, pad(rlo))
        g_ref[hi:, :] = g_ref[hi:, :] - upd


MESH = pl.DeviceIdType.MESH
NB = 8


class Place:
    def __init__(self, height):
        self.m = BLK >> height
        self.leaf = lax.axis_index("leaf")
        self.f = lax.axis_index("front")
        self.core = lax.rem(self.leaf, 2)
        member = lax.rem(self.leaf, 2**height)
        piece = 0
        for bit in range(height):
            piece = piece + lax.rem(member // 2**bit, 2) * 2 ** (height - 1 - bit)
        self.piece = piece
        self.peers = [self.flip(2 * d) for d in range(1, 2 ** (height - 1))]
        self.mate = self.flip(1)

    def flip(self, mask):
        other = self.leaf
        bit = 1
        while bit <= mask:
            if mask & bit:
                other = other + bit * (1 - 2 * lax.rem(self.leaf // bit, 2))
            bit *= 2
        return (other, self.f)

    def greet(self):
        barrier = pltpu.get_barrier_semaphore()
        others = [(self.leaf, lax.rem(self.f + d, NB)) for d in range(1, NB)] + [self.mate] + self.peers
        for other in others:
            pl.semaphore_signal(barrier, inc=1, device_id=other, device_id_type=MESH)
        pl.semaphore_wait(barrier, len(others))


def guarded(conds, body):
    live = [c for c in conds if c is not True]
    if any(c is False for c in live):
        return
    if not live:
        body()
        return
    both = live[0]
    for c in live[1:]:
        both = jnp.logical_and(both, c)
    pl.when(both)(body)


def remote(src, dst, send, recv, device):
    return pltpu.make_async_remote_copy(
        src_ref=src, dst_ref=dst, send_sem=send, recv_sem=recv, device_id=device, device_id_type=MESH
    )


GATHER_SEMS = [pltpu.SemaphoreType.DMA((NB,)) for _ in range(10)]


class Gather:
    def __init__(self, place, buf, sems, lower):
        self.place, self.buf, self.sems, self.lower = place, buf, sems, lower

    def low(self, q):
        return q if self.lower else 0

    def mine(self):
        p = self.place
        return pl.ds(pl.multiple_of(p.piece * p.m, p.m), p.m)

    def half(self):
        return pl.ds(pl.multiple_of(self.place.core * 64, 64), 64)

    def blocks(self, q, rows, count=None):
        lo = self.low(q)
        return self.buf.at[q, pl.ds(lo, NB - lo if count is None else count), rows, :]

    def ring_copy(self, step, q):
        p = self.place
        own = self.buf.at[q, pl.ds(p.f, 1), self.mine(), :]
        to = (p.leaf, lax.rem(p.f + step, NB))
        return remote(own, own, self.sems[0].at[q], self.sems[1].at[q], to)

    def peer_copy(self, d, q):
        own = self.blocks(q, self.mine())
        return remote(own, own, self.sems[2 + d].at[q], self.sems[5].at[q], self.place.peers[d])

    def mate_copy(self, q):
        own = self.blocks(q, self.half())
        return remote(own, own, self.sems[6].at[q], self.sems[7].at[q], self.place.mate)

    def all_of(self, q, sem, count):
        rows = self.buf.at[q, pl.ds(0, count), self.mine(), :]
        return remote(rows, rows, sem, sem, self.place.mate)

    def counted(self, q, sem, count, most, sending):
        def wait(n):
            copy = self.all_of(q, sem, n)
            copy.wait_send() if sending else copy.wait_recv()
        if isinstance(count, int):
            wait(count)
            return
        for n in range(1, most + 1):
            pl.when(count == n)(lambda: wait(n))

    def has(self, origin, q):
        return 1 if self.low(q) == 0 else jnp.where(origin >= q, 1, 0)

    def at(self, step):
        return lax.rem(self.place.f + step, NB)

    def relay_copy(self, origin, step, q):
        own = self.buf.at[q, pl.ds(origin, 1), self.mine(), :]
        return remote(own, own, self.sems[8].at[q], self.sems[9].at[q], (self.place.leaf, self.at(step)))

    def odd(self, q):
        return q % 2 if isinstance(q, int) else lax.rem(q, 2)

    def relay(self, q, *conds):
        def body():
            self.counted(q, self.sems[1].at[q], self.has(self.at(6), q) + self.has(self.at(2), q), 2, False)
            for back, far, parity in ((6, 2, 0), (2, 6, 1)):
                origin = self.at(back)
                def pair():
                    self.relay_copy(origin, 1, q).start()
                    self.relay_copy(origin, 7, q).start()
                    odd = self.odd(q)
                    guarded([odd == parity], lambda: self.relay_copy(origin, far, q).start())
                guarded([True if self.low(q) == 0 else origin >= q], pair)
        guarded([*conds], body)

    def relayed(self, q):
        total = 0
        for step in (1, 3, 4, 5, 7):
            total = total + self.has(self.at(step), q)
        return total

    def relays(self, q):
        left, right = self.has(self.at(6), q), self.has(self.at(2), q)
        return 2 * left + 2 * right + (right if q % 2 else left)

    def holds(self, q):
        return True if self.low(q) == 0 else self.place.f >= q

    def send(self, q, *conds, tree=False):
        def body():
            for step in (2, 6) if tree else (4, 3, 5, 2, 6, 1, 7):
                self.ring_copy(step, q).start()
        guarded([self.holds(q), *conds], body)

    def spread(self, q, *conds, tree=False):
        def body():
            if tree:
                self.counted(q, self.sems[9].at[q], self.relayed(q), 5, False)
            elif self.low(q) == 0:
                self.counted(q, self.sems[1].at[q], NB - 1, 7, False)
            else:
                self.counted(q, self.sems[1].at[q], NB - q - self.has(self.place.f, q), NB - q, False)
            for d in range(len(self.place.peers)):
                self.peer_copy(d, q).start()
            if not self.place.peers:
                self.mate_copy(q).start()
        guarded([*conds], body)

    def cross(self, q, *conds):
        n = len(self.place.peers)
        def body():
            if n == 1:
                self.peer_copy(0, q).wait_recv()
            else:
                lo = self.low(q)
                rows = self.blocks(q, pl.ds(0, n * self.place.m))
                remote(rows, rows, self.sems[5].at[q], self.sems[5].at[q], self.place.mate).wait_recv()
            self.mate_copy(q).start()
        if n:
            guarded([*conds], body)

    def land(self, q):
        self.mate_copy(q).wait_recv()

    def close(self, trees):
        for q in range(NB):
            count = 2 if q in trees else NB - 1
            guarded([self.holds(q)], lambda: self.all_of(q, self.sems[0].at[q], count).wait_send())
            if q in trees:
                self.counted(q, self.sems[8].at[q], self.relays(q), 5, True)
            for d in range(len(self.place.peers)):
                self.peer_copy(d, q).wait_send()
            self.mate_copy(q).wait_send()


def level_kernel(height, update, entries, routes, fac, out, whole, pan, low, got, xh, xl, col, g_ref, u_ref, ex, *sems):
    place = Place(height)
    m = place.m
    f = place.f
    bit = lax.rem(place.leaf // 2 ** (height - 1), 2)
    sibling = place.flip(2 ** (height - 1))
    place.greet()
    out_rows = pl.ds(pl.multiple_of((1 - bit) * m, m), m)
    own_rows = pl.ds(pl.multiple_of(bit * m, m), m)
    swap = remote(update.at[out_rows], got, ex.at[0], ex.at[1], sibling)
    swap.start()
    front = place.leaf // 2**height

    def upper(child, j):
        return jnp.where(routes[front, child, j] >= NB, 1.0, 0.0)

    mine = pl.ds(pl.multiple_of(place.piece * m, m), m)
    row_own = upper(bit, f)
    row_other = upper(1 - bit, f)
    for j in range(NB):
        cols = pl.ds(j * BLK, BLK)
        kept = update[own_rows, cols]
        up = upper(bit, j)
        col[j * m : (j + 1) * m, :] = entries[:m, cols] + ((1.0 - row_own) * (1.0 - up)) * kept
        low[:, cols] = entries[m:, cols] + (row_own * (1.0 - up)) * kept
        out[:, cols] = (row_own * up) * kept
    fac[:m, :] = jnp.zeros((m, 1024), jnp.float32)
    swap.wait()
    for j in range(NB):
        other = got[:, j * BLK : (j + 1) * BLK]
        up = upper(1 - bit, j)
        whole[j, f, mine, :] = col[j * m : (j + 1) * m, :] + ((1.0 - row_other) * (1.0 - up)) * other
    pivots = Gather(place, whole, sems[:10], True)
    panels = Gather(place, pan, sems[10:], False)
    pivots.send(0)
    pivots.send(1)
    for j in range(NB):
        cols = pl.ds(j * BLK, BLK)
        other = got[:, cols]
        up = upper(1 - bit, j)
        low[:, cols] = low[:, cols] + (row_other * (1.0 - up)) * other
        out[:, cols] = out[:, cols] + (row_other * up) * other

    pair = height == 1
    pivot_trees = range(2, NB) if pair else ()
    panel_trees = range(4) if pair else ()
    pivots.spread(0)
    pivots.send(2, tree=pair)
    if not pair:
        pivots.spread(1)
        pivots.cross(0)

    lane = lax.broadcasted_iota(jnp.int32, (BLK, BLK), 1)
    row = lax.broadcasted_iota(jnp.int32, (BLK, BLK), 0)

    def accumulate(q):
        panels.land(q)
        ph, plo = split(fac[m:, pl.ds(pl.multiple_of(q * BLK, BLK), BLK)])
        th, tl = split(pan[q].reshape(1024, BLK))
        out[...] = out[...] - (dott(ph, th) + (dott(ph, tl) + dott(plo, th)))

    plan = {}

    def at(k, half, name, q):
        plan.setdefault((k, half), []).append((name, q))

    if pair:
        at(0, 0, "spread", 1)
        at(0, 1, "relay", 2)
        at(1, 0, "spread", 2)
        for q in range(3, NB):
            at(q - 3, 0, "send", q)
            at(q - 2, 0, "relay", q)
            at(q - 1, 0, "spread", q)
    else:
        at(0, 1, "cross", 1)
        at(0, 1, "spread", 2)
        at(1, 1, "cross", 2)
        for q in range(3, NB):
            at(q - 3, 0, "send", q)
            at(q - 2, 1, "spread", q)
            at(q - 1, 1, "cross", q)

    def slot(k, half):
        for (kk, hh), acts in plan.items():
            if hh == half:
                def go():
                    for name, q in acts:
                        if name in ("send", "spread"):
                            getattr(pivots, name)(q, tree=q in pivot_trees)
                        else:
                            getattr(pivots, name)(q)
                pl.when(k == kk)(go)
        split_at = len(panel_trees)
        if half == 0:
            if pair:
                panels.send(k - 1, k >= 1, k - 1 < split_at, tree=True)
            panels.send(k - 1, k >= 1, k - 1 >= split_at)
            if pair:
                panels.relay(k - 2, k >= 2, k - 2 < split_at)
                panels.spread(k - 3, k >= 3, k - 3 >= split_at)
            pl.when(k >= 4)(lambda: accumulate(k - 4))
        elif pair:
            panels.spread(k - 3, k >= 3, k - 3 < split_at, tree=True)
        else:
            panels.spread(k - 2, k >= 2)
            panels.cross(k - 3, k >= 3)

    def step(k, _):
        for kk in range(NB):
            @pl.when(k == kk)
            def _():
                pivots.land(kk)
                block = whole[kk, kk:, :, :].reshape((NB - kk) * BLK, BLK)
                c = jnp.concatenate([block, low[:, kk * BLK : (kk + 1) * BLK]], 0)
                if kk:
                    K = kk * BLK
                    rh, rl = xh[K : K + BLK, :K], xl[K : K + BLK, :K]
                    c = c - (dott(xh[K:, :K], rh) + (dott(xh[K:, :K], rl) + dott(xl[K:, :K], rh)))
                g_ref[:, :BLK] = c[:BLK]
                col[kk * BLK + BLK :, :] = c[BLK:]
        g_ref[:, BLK:] = jnp.where(lane == row, 1.0, 0.0)
        slot(k, 0)
        for s in range(BLK // SB):
            substep(g_ref, u_ref, s)
            if s == 3:
                slot(k, 1)
        col[pl.ds(pl.multiple_of(k * BLK, BLK), BLK), :] = jnp.where(lane <= row, u_ref[:, :BLK].T, 0.0)
        wh, wl = split(u_ref[:, BLK:])
        for kk in range(NB):
            @pl.when(k == kk)
            def _():
                K = kk * BLK
                ch, cl = split(col[K + BLK :, :])
                x = dott(ch, wh) + (dott(ch, wl) + dott(cl, wh))
                if kk < NB - 1:
                    col[K + BLK : 1024, :] = x[: 1024 - K - BLK]
                tail = x[1024 - K - BLK :]
                fac[m:, K : K + BLK] = tail
                pan[kk, f, mine, :] = tail
                h, l = split(x)
                xh[K + BLK :, K : K + BLK] = h
                xl[K + BLK :, K : K + BLK] = l

        @pl.when(f >= k)
        def _():
            fac[:m, pl.ds(pl.multiple_of(k * BLK, BLK), BLK)] = col[pl.ds(pl.multiple_of(f * BLK + place.piece * m, m), m), :]

        return 0

    lax.fori_loop(0, NB, step, 0)
    panels.send(7)
    accumulate(4)
    if pair:
        panels.spread(5)
        panels.spread(6)
        accumulate(5)
        panels.spread(7)
    else:
        panels.spread(6)
        panels.cross(5)
        accumulate(5)
        panels.spread(7)
        panels.cross(6)
    accumulate(6)
    panels.cross(7)
    accumulate(7)
    pivots.close(pivot_trees)
    panels.close(panel_trees)


def level(height, update, entries, routes):
    m = BLK >> height
    vm = pl.BlockSpec(memory_space=pltpu.VMEM)
    sm = pl.BlockSpec(memory_space=pltpu.SMEM)
    f32, bf16 = jnp.float32, jnp.bfloat16
    return pl.pallas_call(
        functools.partial(level_kernel, height),
        out_shape=(jax.ShapeDtypeStruct((2 * m, 1024), f32), jax.ShapeDtypeStruct((m, 1024), f32)),
        in_specs=[vm, vm, sm],
        out_specs=(vm, vm),
        scratch_shapes=[
            pltpu.VMEM((NB, NB, BLK, BLK), f32),
            pltpu.VMEM((NB, NB, BLK, BLK), f32),
            pltpu.VMEM((m, 1024), f32),
            pltpu.VMEM((m, 1024), f32),
            pltpu.VMEM((1024 + m, 1024), bf16),
            pltpu.VMEM((1024 + m, 1024), bf16),
            pltpu.VMEM((1024 + m, BLK), f32),
            pltpu.VMEM((BLK, 2 * BLK), f32),
            pltpu.VMEM((BLK, 2 * BLK), f32),
            pltpu.SemaphoreType.DMA((2,)),
        ]
        + GATHER_SEMS
        + GATHER_SEMS,
        compiler_params=pltpu.CompilerParams(
            collective_id=height, has_side_effects=True, vmem_limit_bytes=48 * 2**20
        ),
        name="front_level",
    )(update, entries, routes)


def local(
    leaf_contrib,
    entries_lower,
    entries_middle,
    entries_upper,
    assembly_lower,
    assembly_middle,
    assembly_upper,
):
    lower, update = level(1, leaf_contrib, entries_lower, assembly_lower)
    middle, update = level(2, update, entries_middle, assembly_middle)
    upper, update = level(3, update, entries_upper, assembly_upper)
    return (lower, middle, upper, update)


def solution(mesh):
    in_specs = (
        P(("leaf", "front"), None),
        P(("leaf", "front"), None),
        P(("leaf", "front"), None),
        P(("leaf", "front"), None),
        P(),
        P(),
        P(),
    )
    out_specs = (
        P(("leaf", "front"), None),
        P(("leaf", "front"), None),
        P(("leaf", "front"), None),
        P(("leaf", "front"), None),
    )
    return jax.shard_map(local, mesh=mesh, in_specs=in_specs, out_specs=out_specs, check_vma=False)
```

time: 376 us -> 239 us (0.64)
  Pallas kernels: 370 us -> 232 us
    pallas_call x3, Pallas kernels: 370 us -> 232 us  [level(): pl.pallas_call(functools.partial(level_kernel, height), out_shape=(jax.Sh...]
where the time goes in v4:
time: 239 us
  Pallas kernels  232 us (97%)
  local copies, waits for them, and re-layouts  5.66 us (2%)
    pallas_call x3, Pallas kernels, level(): pl.pallas_call(functools.partial(level_kernel, height), out_shape=(jax.Sh...  232 us
    unnamed x17, local copies, waits for them, and re-layouts  5.66 us

profile of v4, /device:TPU:1, one launch (start us, length us, event | category | flops | bytes accessed | tf_op | source)
XLA Modules:
  0.0 238.6 jit_solution(1586632486245798764)
XLA Ops:
  0.6 0.8 copy.11.routes
  1.4 0.0 copy-start
  1.4 1.0 copy-done
  2.5 0.0 copy-start.1
  2.5 1.0 copy-done.1
  3.5 0.0 copy-start.2
  3.5 0.0 copy-start.4
  3.5 83.3 %front_level.3 = (f32[128,1024]{1,0:T(8,128)S(1)}, f32[64,1024]{1,0:T(8,128)S(1)}) custom-call(f32[128,1024]{1,0:T(8,128)S(1)} %copy-done, f32[128,1024]{1,0:T(8,128)S(1)} %copy-done.1, s32[16,2,8]{2,1,0:T(2,128)S(1)} %copy.11.routes), custom_call_target="tpu_custom_call" | custom-call | tf_op jit(solution)/shard_map/front_level/pallas_call | solution.py:441
  86.8 0.0 copy-done.2
  86.8 0.0 copy-done.4
  86.9 0.0 copy-start.3
  86.9 0.0 copy-start.5
  86.9 74.1 %front_level.4 = (f32[64,1024]{1,0:T(8,128)S(1)}, f32[32,1024]{1,0:T(8,128)S(1)}) custom-call(f32[64,1024]{1,0:T(8,128)S(1)} %get-tuple-element.11.update, f32[64,1024]{1,0:T(8,128)S(1)} %copy-done.2, s32[8,2,8]{2,1,0:T(2,128)S(1)} %copy-done.4), custom_call_target="tpu_custom_call" | custom-call | tf_op jit(solution)/shard_map/front_level/pallas_call | solution.py:441
  161.0 0.0 copy-done.3
  161.0 0.0 copy-done.5
  161.0 74.8 %front_level.5 = (f32[32,1024]{1,0:T(8,128)S(1)}, f32[16,1024]{1,0:T(8,128)S(1)}) custom-call(f32[32,1024]{1,0:T(8,128)S(1)} %get-tuple-element.13.update, f32[32,1024]{1,0:T(8,128)S(1)} %copy-done.3, s32[4,2,8]{2,1,0:T(2,128)S(1)} %copy-done.5), custom_call_target="tpu_custom_call" | custom-call | tf_op jit(solution)/shard_map/front_level/pallas_call | solution.py:441
  235.8 0.8 copy.16
  236.6 0.7 copy.17
  237.3 0.7 copy.18
  238.0 0.6 copy.19
Async XLA Ops:
  1.4 1.0 copy-start
  2.5 1.0 copy-start.1
  3.5 83.3 %copy-start.2 = (f32[64,1024]{1,0:T(8,128)S(1)}, f32[64,1024]{1,0:T(8,128)}, u32[]{:S(2)}) copy-start(f32[64,1024]{1,0:T(8,128)} %entries.4) | copy-start | bytes 786436
  3.5 83.4 %copy-start.4 = (s32[8,2,8]{2,1,0:T(2,128)S(1)}, s32[8,2,8]{2,1,0:T(2,128)}, u32[]{:S(2)}) copy-start(s32[8,2,8]{2,1,0:T(2,128)} %routes.3) | copy-start | bytes 1540
  86.9 74.1 %copy-start.3 = (f32[32,1024]{1,0:T(8,128)S(1)}, f32[32,1024]{1,0:T(8,128)}, u32[]{:S(2)}) copy-start(f32[32,1024]{1,0:T(8,128)} %entries.5) | copy-start | bytes 393220
  86.9 74.1 %copy-start.5 = (s32[4,2,8]{2,1,0:T(2,128)S(1)}, s32[4,2,8]{2,1,0:T(2,128)}, u32[]{:S(2)}) copy-start(s32[4,2,8]{2,1,0:T(2,128)} %routes.4) | copy-start | bytes 772

commit v5 on v4

--- a/solution.py
+++ b/solution.py
@@ -105,7 +105,20 @@
         others = [(self.leaf, lax.rem(self.f + d, NB)) for d in range(1, NB)] + [self.mate] + self.peers
         for other in others:
             pl.semaphore_signal(barrier, inc=1, device_id=other, device_id_type=MESH)
-        pl.semaphore_wait(barrier, len(others))
+        n = len(self.peers)
+        if n == 0:
+            pl.semaphore_wait(barrier, len(others))
+            return
+        for leaf, _ in self.peers:
+            @pl.when(self.f != 0)
+            def _():
+                pl.semaphore_signal(barrier, inc=1, device_id=(leaf, 0), device_id_type=MESH)
+        @pl.when(self.f != 0)
+        def _():
+            pl.semaphore_wait(barrier, len(others))
+        @pl.when(self.f == 0)
+        def _():
+            pl.semaphore_wait(barrier, len(others) + (NB - 1) * n)
 
 
 def guarded(conds, body):
@@ -135,7 +148,7 @@
         self.place, self.buf, self.sems, self.lower = place, buf, sems, lower
 
     def low(self, q):
-        return q if self.lower else 0
+        return max(q, 1) if self.lower else 0
 
     def mine(self):
         p = self.place
@@ -177,7 +190,7 @@
             pl.when(count == n)(lambda: wait(n))
 
     def has(self, origin, q):
-        return 1 if self.low(q) == 0 else jnp.where(origin >= q, 1, 0)
+        return 1 if self.low(q) == 0 else jnp.where(origin >= self.low(q), 1, 0)
 
     def at(self, step):
         return lax.rem(self.place.f + step, NB)
@@ -199,7 +212,7 @@
                     self.relay_copy(origin, 7, q).start()
                     odd = self.odd(q)
                     guarded([odd == parity], lambda: self.relay_copy(origin, far, q).start())
-                guarded([True if self.low(q) == 0 else origin >= q], pair)
+                guarded([True if self.low(q) == 0 else origin >= self.low(q)], pair)
         guarded([*conds], body)
 
     def relayed(self, q):
@@ -213,7 +226,7 @@
         return 2 * left + 2 * right + (right if q % 2 else left)
 
     def holds(self, q):
-        return True if self.low(q) == 0 else self.place.f >= q
+        return True if self.low(q) == 0 else self.place.f >= self.low(q)
 
     def send(self, q, *conds, tree=False):
         def body():
@@ -228,7 +241,7 @@
             elif self.low(q) == 0:
                 self.counted(q, self.sems[1].at[q], NB - 1, 7, False)
             else:
-                self.counted(q, self.sems[1].at[q], NB - q - self.has(self.place.f, q), NB - q, False)
+                self.counted(q, self.sems[1].at[q], NB - self.low(q) - self.has(self.place.f, q), NB - self.low(q), False)
             for d in range(len(self.place.peers)):
                 self.peer_copy(d, q).start()
             if not self.place.peers:
@@ -262,7 +275,55 @@
             self.mate_copy(q).wait_send()
 
 
-def level_kernel(height, update, entries, routes, fac, out, whole, pan, low, got, xh, xl, col, g_ref, u_ref, ex, *sems):
+class Seed:
+    def __init__(self, place, buf, sems):
+        self.place, self.sems, self.block = place, sems, buf.at[0, 0]
+        self.owner = place.f == 0
+        self.mine = self.block.at[pl.ds(pl.multiple_of(place.piece * place.m, place.m), place.m), :]
+
+    def sized(self, count, send, recv):
+        rows = self.block.at[pl.ds(0, count), :]
+        return remote(rows, rows, send, recv, self.place.mate)
+
+    def send(self):
+        p = self.place
+        def body():
+            for step in (4, 3, 5, 2, 6, 1, 7):
+                for leaf in [p.leaf] + [peer[0] for peer in p.peers]:
+                    to = (leaf, lax.rem(p.f + step, NB))
+                    remote(self.mine, self.mine, self.sems.at[0], self.sems.at[2], to).start()
+            for peer in p.peers:
+                remote(self.mine, self.mine, self.sems.at[1], self.sems.at[2], peer).start()
+        pl.when(self.owner)(body)
+
+    def forward(self):
+        p = self.place
+        n = len(p.peers)
+        sem = self.sems.at[2]
+        if n:
+            pl.when(self.owner)(lambda: self.sized(n * p.m, sem, sem).wait_recv())
+        pl.when(jnp.logical_not(self.owner))(lambda: self.sized(64, sem, sem).wait_recv())
+        self.mate_copy().start()
+
+    def mate_copy(self):
+        half = self.block.at[pl.ds(pl.multiple_of(self.place.core * 64, 64), 64), :]
+        return remote(half, half, self.sems.at[3], self.sems.at[4], self.place.mate)
+
+    def land(self):
+        self.mate_copy().wait_recv()
+
+    def close(self, buf):
+        p = self.place
+        def body():
+            rows = buf.at[0, pl.ds(0, NB - 1), pl.ds(0, 64), :]
+            remote(rows, rows, self.sems.at[0], self.sems.at[0], p.mate).wait_send()
+            if p.peers:
+                self.sized(len(p.peers) * p.m, self.sems.at[1], self.sems.at[1]).wait_send()
+        pl.when(self.owner)(body)
+        self.mate_copy().wait_send()
+
+
+def level_kernel(height, update, entries, routes, fac, out, whole, pan, low, got, xh, xl, col, g_ref, u_ref, ex, early, *sems):
     place = Place(height)
     m = place.m
     f = place.f
@@ -296,6 +357,8 @@
         whole[j, f, mine, :] = col[j * m : (j + 1) * m, :] + ((1.0 - row_other) * (1.0 - up)) * other
     pivots = Gather(place, whole, sems[:10], True)
     panels = Gather(place, pan, sems[10:], False)
+    seed = Seed(place, whole, early)
+    seed.send()
     pivots.send(0)
     pivots.send(1)
     for j in range(NB):
@@ -308,11 +371,14 @@
     pair = height == 1
     pivot_trees = range(2, NB) if pair else ()
     panel_trees = range(4) if pair else ()
-    pivots.spread(0)
-    pivots.send(2, tree=pair)
+    pair = height == 1
+    pivot_trees = range(2, NB) if pair else ()
+    panel_trees = range(6) if pair else ()
+    seed.forward()
     if not pair:
-        pivots.spread(1)
-        pivots.cross(0)
+        pivots.spread(0)
+        pivots.send(2)
+    seed.land()
 
     lane = lax.broadcasted_iota(jnp.int32, (BLK, BLK), 1)
     row = lax.broadcasted_iota(jnp.int32, (BLK, BLK), 0)
@@ -329,19 +395,23 @@
         plan.setdefault((k, half), []).append((name, q))
 
     if pair:
+        at(0, 1, "spread", 0)
+        at(0, 1, "send", 2)
+        at(0, 2, "spread", 1)
+        at(1, 0, "relay", 2)
+        at(1, 2, "spread", 2)
+        for q in range(3, NB):
+            at(q - 3, 1, "send", q)
+            at(q - 2, 1, "relay", q)
+            at(q - 1, 1, "spread", q)
+    else:
         at(0, 0, "spread", 1)
-        at(0, 1, "relay", 2)
-        at(1, 0, "spread", 2)
-        for q in range(3, NB):
-            at(q - 3, 0, "send", q)
-            at(q - 2, 0, "relay", q)
-            at(q - 1, 0, "spread", q)
-    else:
-        at(0, 1, "cross", 1)
-        at(0, 1, "spread", 2)
+        at(0, 1, "cross", 0)
+        at(0, 2, "cross", 1)
+        at(0, 2, "spread", 2)
         at(1, 1, "cross", 2)
         for q in range(3, NB):
-            at(q - 3, 0, "send", q)
+            at(q - 3, 1, "send", q)
             at(q - 2, 1, "spread", q)
             at(q - 1, 1, "cross", q)
 
@@ -362,11 +432,10 @@
             panels.send(k - 1, k >= 1, k - 1 >= split_at)
             if pair:
                 panels.relay(k - 2, k >= 2, k - 2 < split_at)
-                panels.spread(k - 3, k >= 3, k - 3 >= split_at)
             pl.when(k >= 4)(lambda: accumulate(k - 4))
-        elif pair:
+        elif half == 1 and pair:
             panels.spread(k - 3, k >= 3, k - 3 < split_at, tree=True)
-        else:
+        elif half == 1:
             panels.spread(k - 2, k >= 2)
             panels.cross(k - 3, k >= 3)
 
@@ -374,6 +443,9 @@
         for kk in range(NB):
             @pl.when(k == kk)
             def _():
+                if kk == 0:
+                    g_ref[:, :BLK] = whole[0, 0]
+                    return
                 pivots.land(kk)
                 block = whole[kk, kk:, :, :].reshape((NB - kk) * BLK, BLK)
                 c = jnp.concatenate([block, low[:, kk * BLK : (kk + 1) * BLK]], 0)
@@ -389,12 +461,17 @@
             substep(g_ref, u_ref, s)
             if s == 3:
                 slot(k, 1)
+        slot(k, 2)
         col[pl.ds(pl.multiple_of(k * BLK, BLK), BLK), :] = jnp.where(lane <= row, u_ref[:, :BLK].T, 0.0)
         wh, wl = split(u_ref[:, BLK:])
         for kk in range(NB):
             @pl.when(k == kk)
             def _():
                 K = kk * BLK
+                if kk == 0:
+                    pivots.land(0)
+                    col[BLK:1024, :] = whole[0, 1:].reshape(1024 - BLK, BLK)
+                    col[1024:, :] = low[:, :BLK]
                 ch, cl = split(col[K + BLK :, :])
                 x = dott(ch, wh) + (dott(ch, wl) + dott(cl, wh))
                 if kk < NB - 1:
@@ -416,7 +493,7 @@
     panels.send(7)
     accumulate(4)
     if pair:
-        panels.spread(5)
+        panels.spread(5, tree=True)
         panels.spread(6)
         accumulate(5)
         panels.spread(7)
@@ -429,6 +506,7 @@
     accumulate(6)
     panels.cross(7)
     accumulate(7)
+    seed.close(whole)
     pivots.close(pivot_trees)
     panels.close(panel_trees)
 
@@ -454,6 +532,7 @@
             pltpu.VMEM((BLK, 2 * BLK), f32),
             pltpu.VMEM((BLK, 2 * BLK), f32),
             pltpu.SemaphoreType.DMA((2,)),
+            pltpu.SemaphoreType.DMA((5,)),
         ]
         + GATHER_SEMS
         + GATHER_SEMS,

time: 239 us -> 233 us (0.975)
  Pallas kernels: 232 us -> 226 us
    pallas_call x3, Pallas kernels: 232 us -> 226 us  [level(): pl.pallas_call(functools.partial(level_kernel, height), out_shape=(jax.Sh...]
where the time goes in v5:
time: 233 us; the launch traced here: 232 us
  Pallas kernels  226 us (97%)
  local copies, waits for them, and re-layouts  5.66 us (2%)
    pallas_call x3, Pallas kernels, level(): pl.pallas_call(functools.partial(level_kernel, height), out_shape=(jax.Sh...  226 us
    unnamed x17, local copies, waits for them, and re-layouts  5.66 us

profile of v5, /device:TPU:1, one launch (start us, length us, event | category | flops | bytes accessed | tf_op | source)
XLA Modules:
  0.0 232.4 jit_solution(3454815973797439140)
XLA Ops:
  0.6 0.8 copy.11.routes
  1.4 0.0 copy-start
  1.4 1.0 copy-done
  2.5 0.0 copy-start.1
  2.5 1.0 copy-done.1
  3.5 0.0 copy-start.2
  3.5 0.0 copy-start.4
  3.5 80.9 %front_level.3 = (f32[128,1024]{1,0:T(8,128)S(1)}, f32[64,1024]{1,0:T(8,128)S(1)}) custom-call(f32[128,1024]{1,0:T(8,128)S(1)} %copy-done, f32[128,1024]{1,0:T(8,128)S(1)} %copy-done.1, s32[16,2,8]{2,1,0:T(2,128)S(1)} %copy.11.routes), custom_call_target="tpu_custom_call" | custom-call | tf_op jit(solution)/shard_map/front_level/pallas_call | solution.py:519
  84.4 0.0 copy-done.2
  84.4 0.0 copy-done.4
  84.4 0.0 copy-start.3
  84.5 0.0 copy-start.5
  84.5 73.4 %front_level.4 = (f32[64,1024]{1,0:T(8,128)S(1)}, f32[32,1024]{1,0:T(8,128)S(1)}) custom-call(f32[64,1024]{1,0:T(8,128)S(1)} %get-tuple-element.11.update, f32[64,1024]{1,0:T(8,128)S(1)} %copy-done.2, s32[8,2,8]{2,1,0:T(2,128)S(1)} %copy-done.4), custom_call_target="tpu_custom_call" | custom-call | tf_op jit(solution)/shard_map/front_level/pallas_call | solution.py:519
  157.9 0.0 copy-done.3
  157.9 0.0 copy-done.5
  157.9 71.7 %front_level.5 = (f32[32,1024]{1,0:T(8,128)S(1)}, f32[16,1024]{1,0:T(8,128)S(1)}) custom-call(f32[32,1024]{1,0:T(8,128)S(1)} %get-tuple-element.13.update, f32[32,1024]{1,0:T(8,128)S(1)} %copy-done.3, s32[4,2,8]{2,1,0:T(2,128)S(1)} %copy-done.5), custom_call_target="tpu_custom_call" | custom-call | tf_op jit(solution)/shard_map/front_level/pallas_call | solution.py:519
  229.6 0.8 copy.16
  230.4 0.7 copy.17
  231.1 0.7 copy.18
  231.8 0.6 copy.19
Async XLA Ops:
  1.4 1.0 copy-start
  2.5 1.0 copy-start.1
  3.5 80.9 %copy-start.2 = (f32[64,1024]{1,0:T(8,128)S(1)}, f32[64,1024]{1,0:T(8,128)}, u32[]{:S(2)}) copy-start(f32[64,1024]{1,0:T(8,128)} %entries.4) | copy-start | bytes 786436
  3.5 80.9 %copy-start.4 = (s32[8,2,8]{2,1,0:T(2,128)S(1)}, s32[8,2,8]{2,1,0:T(2,128)}, u32[]{:S(2)}) copy-start(s32[8,2,8]{2,1,0:T(2,128)} %routes.3) | copy-start | bytes 1540
  84.4 73.4 %copy-start.3 = (f32[32,1024]{1,0:T(8,128)S(1)}, f32[32,1024]{1,0:T(8,128)}, u32[]{:S(2)}) copy-start(f32[32,1024]{1,0:T(8,128)} %entries.5) | copy-start | bytes 393220
  84.5 73.4 %copy-start.5 = (s32[4,2,8]{2,1,0:T(2,128)S(1)}, s32[4,2,8]{2,1,0:T(2,128)}, u32[]{:S(2)}) copy-start(s32[4,2,8]{2,1,0:T(2,128)} %routes.4) | copy-start | bytes 772

commit v6 on v5

--- a/solution.py
+++ b/solution.py
@@ -411,8 +411,12 @@
         at(0, 2, "spread", 2)
         at(1, 1, "cross", 2)
         for q in range(3, NB):
-            at(q - 3, 1, "send", q)
-            at(q - 2, 1, "spread", q)
+            if height == 3:
+                at(0, 0 if q < 5 else 1, "send", q)
+                at(q - 2, 0, "spread", q)
+            else:
+                at(q - 3, 1, "send", q)
+                at(q - 2, 1, "spread", q)
             at(q - 1, 1, "cross", q)
 
     def slot(k, half):

time: 233 us -> 232 us (level)
  no operation moved by 1% of the time
where the time goes in v6:
time: 232 us; the launch traced here: 231 us
  Pallas kernels  225 us (97%)
  local copies, waits for them, and re-layouts  5.66 us (2%)
    pallas_call x3, Pallas kernels, level(): pl.pallas_call(functools.partial(level_kernel, height), out_shape=(jax.Sh...  225 us
    unnamed x17, local copies, waits for them, and re-layouts  5.66 us

profile of v6, /device:TPU:1, one launch (start us, length us, event | category | flops | bytes accessed | tf_op | source)
XLA Modules:
  0.0 230.9 jit_solution(10955332791132219422)
XLA Ops:
  0.6 0.8 copy.11.routes
  1.4 0.0 copy-start
  1.4 1.0 copy-done
  2.5 0.0 copy-start.1
  2.5 1.0 copy-done.1
  3.5 0.0 copy-start.2
  3.5 0.0 copy-start.4
  3.5 80.9 %front_level.3 = (f32[128,1024]{1,0:T(8,128)S(1)}, f32[64,1024]{1,0:T(8,128)S(1)}) custom-call(f32[128,1024]{1,0:T(8,128)S(1)} %copy-done, f32[128,1024]{1,0:T(8,128)S(1)} %copy-done.1, s32[16,2,8]{2,1,0:T(2,128)S(1)} %copy.11.routes), custom_call_target="tpu_custom_call" | custom-call | tf_op jit(solution)/shard_map/front_level/pallas_call | solution.py:523
  84.4 0.0 copy-done.2
  84.4 0.0 copy-done.4
  84.4 0.0 copy-start.3
  84.5 0.0 copy-start.5
  84.5 73.4 %front_level.4 = (f32[64,1024]{1,0:T(8,128)S(1)}, f32[32,1024]{1,0:T(8,128)S(1)}) custom-call(f32[64,1024]{1,0:T(8,128)S(1)} %get-tuple-element.11.update, f32[64,1024]{1,0:T(8,128)S(1)} %copy-done.2, s32[8,2,8]{2,1,0:T(2,128)S(1)} %copy-done.4), custom_call_target="tpu_custom_call" | custom-call | tf_op jit(solution)/shard_map/front_level/pallas_call | solution.py:523
  157.9 0.0 copy-done.3
  157.9 0.0 copy-done.5
  157.9 70.2 %front_level.5 = (f32[32,1024]{1,0:T(8,128)S(1)}, f32[16,1024]{1,0:T(8,128)S(1)}) custom-call(f32[32,1024]{1,0:T(8,128)S(1)} %get-tuple-element.13.update, f32[32,1024]{1,0:T(8,128)S(1)} %copy-done.3, s32[4,2,8]{2,1,0:T(2,128)S(1)} %copy-done.5), custom_call_target="tpu_custom_call" | custom-call | tf_op jit(solution)/shard_map/front_level/pallas_call | solution.py:523
  228.1 0.8 copy.16
  228.9 0.7 copy.17
  229.6 0.7 copy.18
  230.3 0.6 copy.19
Async XLA Ops:
  1.4 1.0 copy-start
  2.5 1.0 copy-start.1
  3.5 80.9 %copy-start.2 = (f32[64,1024]{1,0:T(8,128)S(1)}, f32[64,1024]{1,0:T(8,128)}, u32[]{:S(2)}) copy-start(f32[64,1024]{1,0:T(8,128)} %entries.4) | copy-start | bytes 786436
  3.5 80.9 %copy-start.4 = (s32[8,2,8]{2,1,0:T(2,128)S(1)}, s32[8,2,8]{2,1,0:T(2,128)}, u32[]{:S(2)}) copy-start(s32[8,2,8]{2,1,0:T(2,128)} %routes.3) | copy-start | bytes 1540
  84.4 73.4 %copy-start.3 = (f32[32,1024]{1,0:T(8,128)S(1)}, f32[32,1024]{1,0:T(8,128)}, u32[]{:S(2)}) copy-start(f32[32,1024]{1,0:T(8,128)} %entries.5) | copy-start | bytes 393220
  84.5 73.4 %copy-start.5 = (s32[4,2,8]{2,1,0:T(2,128)S(1)}, s32[4,2,8]{2,1,0:T(2,128)}, u32[]{:S(2)}) copy-start(s32[4,2,8]{2,1,0:T(2,128)} %routes.4) | copy-start | bytes 772
